TPU v7x, 32 devices: a whole 2x2x4 slice. The times are simulated.
32 devices in a mesh: grp: 2 (over y), pre: 4 (over z), row: 4 (over x, core).
Axes of the slice: x: 2, y: 2, z: 4, core: 2. Of those that a mesh axis runs over, the one named last changes fastest.
Arguments:
- queries: bfloat16 [32, 2, 8192], P(('grp', 'row')), parts along dimension 0, may hold values from -200 to 200
- prefix_keys: bfloat16 [1024, 1024], P(('grp', 'pre')), parts along dimension 0, may hold values from -7 to 7
- prefix_values: bfloat16 [1024, 1024], P(('grp', 'pre')), parts along dimension 0, may hold values from -6 to 6
- suffix_keys: bfloat16 [32, 64, 1024], P(('grp', 'row'), 'pre'), parts along dimension 0, may hold values from -6 to 6
- suffix_values: bfloat16 [32, 64, 1024], P(('grp', 'row'), 'pre'), parts along dimension 0, may hold values from -6 to 6
- new_keys: bfloat16 [32, 2, 1024], P(('grp', 'row')), parts along dimension 0, may hold values from -6 to 6
- new_values: bfloat16 [32, 2, 1024], P(('grp', 'row')), parts along dimension 0, may hold values from -6 to 6
- hidden: bfloat16 [32, 2, 8192], P(('grp', 'pre'), None, 'row'), parts along dimension 0, may hold values from -6 to 6
- adapter_ids: int32 [32], P(('grp', 'row')), parts along dimension 0, may hold values from 0 to 127
- suffix_lengths: int32 [32], P(('grp', 'row')), parts along dimension 0, may hold values from 1 to 64
- kv_scales: bfloat16 [128, 2, 1024], replicated, may hold values from 0.25 to 1.75
- ffn_scales: bfloat16 [128, 14336], P(None, 'pre'), may hold values from 0.25 to 1.75
- out_weight: bfloat16 [8192, 8192], P('pre', 'row'), may hold values from -0.0625 to 0.0625
- norm_gain: bfloat16 [8192], P('row'), may hold values from 0.25 to 1.75
- gate_up: bfloat16 [8192, 2, 14336], P('row', None, 'pre'), may hold values from -0.0625 to 0.0625
Outputs:
- residual: bfloat16 [32, 2, 8192], P(('grp', 'pre'), None, 'row'), parts along dimension 0
- activation: bfloat16 [32, 2, 14336], P(('grp', 'row'), None, 'pre'), parts along dimension 0
There are 2 independent parts, one for each index of `grp`. A program takes and returns all parts, laid end to end along the dimension named above; an argument that names none is the same for every part. Nothing has to cross between parts.
All inputs are finite; a program needn't handle non-finite values.
Results may differ from a plain program's by a relative error of at most 0.015.
Values may be sent and summed in bfloat16 or wider, within the bound.
A program may use at most 128 MiB of HBM per device.

v0:
```python
import functools

import jax
import jax.numpy as jnp
from jax import lax
from jax.experimental import pallas as pl
from jax.experimental.pallas import tpu as pltpu
from jax.sharding import PartitionSpec as P

D = 8192
HEADS = 64
KV_HEADS = 8
HD = 128
STEPS = 2
GROUP = HEADS // KV_HEADS
LANES = 128
FFN_GROUPS = 7

masked_score = -1e30
f32 = jnp.float32
bf16 = jnp.bfloat16


def iota(shape, axis):
    return lax.broadcasted_iota(jnp.int32, shape, axis)


def layer_kernel(
    sizes,
    ids_ref,
    lens_ref,
    q_ref,
    pk_ref,
    pv_ref,
    sk_ref,
    sv_ref,
    nk_ref,
    nv_ref,
    hid_ref,
    kvs_ref,
    gain_ref,
    ffs_hbm,
    ow_hbm,
    gu_hbm,
    res_out,
    act_out,
    ow,
    gu,
    ffs,
    q8,
    ks8,
    vs8,
    fk8,
    fv8,
    acc_s,
    acc_r,
    stat_s,
    stat_r,
    mix_g,
    mix_x,
    prod_s,
    prod_f,
    prod_r,
    res_g,
    x_exp,
    gate_s,
    gate_f,
    gate_r,
    sq_s,
    sq_r,
    ffn8,
    ow_sem,
    gu_sem,
    ffs_sem,
    acc_sem,
    stat_sem,
    mix_sem,
    prod_sem,
    res_sem,
    pass_sem,
    gate_sem,
    sq_sem,
):
    pre_n, row_n, split = sizes
    grp = lax.rem(lax.axis_index("grp"), split)
    pre = lax.axis_index("pre")
    row = lax.axis_index("row")
    row_local = q_ref.shape[0]
    rs = row_local * STEPS
    hid_local = hid_ref.shape[0]
    hs = hid_local * STEPS
    suffix_local = sk_ref.shape[1]
    kv_width = pk_ref.shape[1]
    adapters = kvs_ref.shape[0]
    block = D // pre_n
    heads_block = block // HD
    cols = ow_hbm.shape[1]
    depth = gu_hbm.shape[0]
    ff = gu_hbm.shape[2]
    score_scale = HD ** (-0.5)
    n_out, _, out_width = ow.shape
    n_tiles = gu.shape[0]
    share = n_tiles * LANES
    group_width = gate_s.shape[4]
    tiles_group = n_tiles // FFN_GROUPS
    everyone = row_n * rs

    def ow_copy(c):
        return pltpu.make_async_copy(
            ow_hbm.at[:, pl.ds(c * out_width, out_width)], ow.at[c], ow_sem.at[c]
        )

    def gu_copy(c):
        return pltpu.make_async_copy(
            gu_hbm.at[:, :, pl.ds(pl.multiple_of(grp * share + c * LANES, LANES), LANES)], gu.at[c], gu_sem.at[c]
        )

    ffs_copy = pltpu.make_async_copy(ffs_hbm, ffs, ffs_sem)
    for c in range(n_out):
        ow_copy(c).start()
    ffs_copy.start()
    for c in range(n_tiles):
        gu_copy(c).start()

    barrier = pltpu.get_barrier_semaphore()
    for d in range(1, pre_n):
        pl.semaphore_signal(
            barrier,
            inc=1,
            device_id={"pre": lax.rem(pre + d, pre_n)},
            device_id_type=pl.DeviceIdType.MESH,
        )
    for d in range(1, row_n):
        pl.semaphore_signal(
            barrier,
            inc=1,
            device_id={"row": lax.rem(row + d, row_n)},
            device_id_type=pl.DeviceIdType.MESH,
        )
    for e in range(1, split):
        for d in range(row_n):
            pl.semaphore_signal(
                barrier,
                inc=1,
                device_id={"grp": lax.rem(grp + e, split), "row": lax.rem(row + d, row_n)},
                device_id_type=pl.DeviceIdType.MESH,
            )

    def remote(src, dst, sems, axis, target, group=None):
        return pltpu.make_async_remote_copy(
            src_ref=src,
            dst_ref=dst,
            send_sem=sems[0],
            recv_sem=sems[1],
            device_id={axis: target} if group is None else {"grp": group, axis: target},
            device_id_type=pl.DeviceIdType.MESH,
        )

    def pair(sem, *at):
        return sem.at[(0,) + at], sem.at[(1,) + at]

    def ahead(d):
        return lax.rem(pre + d, pre_n)

    def beside(d):
        return lax.rem(row + d, row_n)

    def acc_copy(d):
        return remote(acc_s.at[ahead(d)], acc_r.at[d - 1], pair(acc_sem, d - 1), "pre", ahead(d))

    def stat_copy(d):
        return remote(stat_s.at[ahead(d)], stat_r.at[d - 1], pair(stat_sem, d - 1), "pre", ahead(d))

    def mix_copy(d):
        return remote(mix_g.at[row], mix_g.at[row], pair(mix_sem, d - 1), "row", beside(d))

    def prod_copy(c, d):
        return remote(
            prod_s.at[c, ahead(d)], prod_r.at[c, d - 1], pair(prod_sem, c, d - 1), "pre", ahead(d)
        )

    def res_copy(d):
        block_at = res_g.at[grp, pre]
        return remote(block_at, block_at, pair(res_sem, d - 1), "pre", ahead(d))

    def across(e):
        return lax.rem(grp + e, split)

    def pass_copy(e, d):
        block_at = res_g.at[grp, lax.rem(pre + pre_n - d, pre_n)]
        return remote(block_at, block_at, pair(pass_sem, e - 1, d), "grp", across(e))

    def sq_copy(d):
        return remote(sq_s.at[beside(d)], sq_r.at[d - 1], pair(sq_sem, d - 1), "row", beside(d))

    def gate_copy(g, e, d):
        return remote(
            gate_s.at[g, e, beside(d)],
            gate_r.at[g, e, d],
            pair(gate_sem, g, e, d),
            "row",
            beside(d),
            across(e) if e > 0 else None,
        )

    others = [(e, d) for e in range(split) for d in range(row_n) if e + d > 0]

    def per_row(ref, shape):
        which = iota(shape, 0) // STEPS
        out = jnp.full(shape, ref[0], jnp.int32)
        for r in range(1, row_local):
            out = jnp.where(which == r, ref[r], out)
        return out

    adapter = per_row(ids_ref, (rs, 2 * adapters))
    lane = iota((rs, 2 * adapters), 1)
    pick_key = jnp.where(lane == 2 * adapter, 1.0, 0.0)
    pick_value = jnp.where(lane == 2 * adapter + 1, 1.0, 0.0)
    pick = jnp.concatenate([pick_key, pick_value], axis=0).astype(bf16)
    scales = jnp.dot(
        pick, kvs_ref[...].reshape(2 * adapters, kv_width), preferred_element_type=f32
    )
    ks8[...] = scales[:rs]
    vs8[...] = scales[rs:]
    fk8[...] = nk_ref[...].astype(f32).reshape(rs, kv_width) * scales[:rs]
    fv8[...] = nv_ref[...].astype(f32).reshape(rs, kv_width) * scales[rs:]
    q8[...] = q_ref[...].astype(f32).reshape(rs, D)

    unit_heads = min(GROUP, heads_block)
    units = heads_block // unit_heads
    unit_rows = unit_heads * rs
    suffix_rows = row_local * suffix_local
    own_rows = -(-(suffix_rows + rs) // LANES) * LANES
    pad = own_rows - suffix_rows - rs
    at_row = lax.rem(iota((unit_rows, own_rows), 0), rs)
    at_col = iota((unit_rows, own_rows), 1)
    lens = per_row(lens_ref, (rs, own_rows))
    lens = jnp.concatenate([lens] * unit_heads, axis=0)
    query_row = at_row // STEPS
    query_step = lax.rem(at_row, STEPS)
    position = pre * suffix_local + lax.rem(at_col, suffix_local)
    fresh_at = at_col - suffix_rows
    in_suffix = (at_col < suffix_rows) & (at_col // suffix_local == query_row) & (position < lens)
    in_new = (
        (fresh_at >= 0)
        & (fresh_at < rs)
        & (fresh_at // STEPS == query_row)
        & (lax.rem(fresh_at, STEPS) <= query_step)
        & (pre == 0)
    )
    mask = in_suffix | in_new
    stat_lane = iota((rs, LANES), 1)
    transposed = (((1,), (1,)), ((), ()))

    def with_fresh(old, fresh):
        tail = jnp.concatenate([fresh, jnp.zeros((pad, HD), f32)], axis=0) if pad else fresh
        return jnp.concatenate([old.reshape(suffix_rows, HD), tail.astype(bf16)], axis=0)

    def attend(b, finish):
        peaks = jnp.zeros((rs, LANES), f32)
        totals = jnp.ones((rs, LANES), f32)
        for i in range(units):
            first = b * heads_block + i * unit_heads
            kv = pl.ds(pl.multiple_of(first // GROUP * HD, HD), HD)
            pieces = [
                q8[:, pl.ds(pl.multiple_of((first + g) * HD, HD), HD)] for g in range(unit_heads)
            ]
            key_scale = ks8[:, kv]
            value_scale = vs8[:, kv]
            query = jnp.concatenate(pieces, axis=0).astype(bf16)
            scaled = jnp.concatenate([piece * key_scale for piece in pieces], axis=0).astype(bf16)
            own_keys = with_fresh(sk_ref[:, :, kv], fk8[:, kv])
            own_values = with_fresh(sv_ref[:, :, kv], fv8[:, kv])
            prefix_scores = (
                lax.dot_general(scaled, pk_ref[:, kv], transposed, preferred_element_type=f32)
                * score_scale
            )
            own_scores = (
                lax.dot_general(query, own_keys, transposed, preferred_element_type=f32)
                * score_scale
            )
            own_scores = jnp.where(mask, own_scores, masked_score)
            peak = jnp.maximum(
                jnp.max(prefix_scores, axis=1, keepdims=True),
                jnp.max(own_scores, axis=1, keepdims=True),
            )
            prefix_weight = jnp.exp(prefix_scores - peak).astype(bf16)
            own_weight = jnp.where(mask, jnp.exp(own_scores - peak), 0.0).astype(bf16)
            total = jnp.sum(prefix_weight.astype(f32), axis=1, keepdims=True) + jnp.sum(
                own_weight.astype(f32), axis=1, keepdims=True
            )
            numerator = jnp.dot(prefix_weight, pv_ref[:, kv], preferred_element_type=f32)
            numerator = numerator * jnp.concatenate([value_scale] * unit_heads, axis=0)
            numerator = numerator + jnp.dot(own_weight, own_values, preferred_element_type=f32)
            for g in range(unit_heads):
                j = i * unit_heads + g
                part = slice(g * rs, (g + 1) * rs)
                peaks = jnp.where(stat_lane == j, peak[part], peaks)
                totals = jnp.where(stat_lane == j, total[part], totals)
                acc_s[b, :, j * HD : (j + 1) * HD] = numerator[part].astype(bf16)
        stat_s[b, 0] = peaks
        stat_s[b, 1] = totals
        finish()

    for d in list(range(1, pre_n)) + [0]:

        def finish(d=d):
            if d == 1:
                pl.semaphore_wait(barrier, pre_n + row_n - 2 + (split - 1) * row_n)
            if d > 0:
                stat_copy(d).start()
                acc_copy(d).start()

        attend(ahead(d), finish)

    ffs_copy.wait()
    ffn_pick = jnp.where(
        iota((rs, adapters), 1) == per_row(ids_ref, (rs, adapters)), 1.0, 0.0
    ).astype(bf16)
    ffn8[...] = jnp.dot(ffn_pick, ffs[...], preferred_element_type=f32)

    for d in range(1, pre_n):
        stat_copy(d).wait_recv()
    peak_of = [stat_s[pre, 0]] + [stat_r[d - 1, 0] for d in range(1, pre_n)]
    total_of = [stat_s[pre, 1]] + [stat_r[d - 1, 1] for d in range(1, pre_n)]
    highest = functools.reduce(jnp.maximum, peak_of)
    factor_of = [jnp.exp(peak - highest) for peak in peak_of]
    weight_sum = sum(factor * total for factor, total in zip(factor_of, total_of))
    factor_of = [factor / weight_sum for factor in factor_of]
    for d in range(1, pre_n):
        acc_copy(d).wait_recv()
    for j in range(heads_block):
        part = slice(j * HD, (j + 1) * HD)
        value = acc_s[pre, :, part].astype(f32) * factor_of[0][:, j : j + 1]
        for d in range(1, pre_n):
            value = value + acc_r[d - 1, :, part].astype(f32) * factor_of[d][:, j : j + 1]
        mix_g[row, :, part] = value.astype(bf16)
    for d in range(1, row_n):
        mix_copy(d).start()
    for c in range(n_out):
        ow_copy(c).wait()
    for d in range(1, row_n):
        mix_copy(d).wait_recv()
    mix_x[...] = mix_g[...].astype(f32).reshape(everyone, block).astype(bf16)

    def project(c, carry):
        product = jnp.dot(mix_x[...], ow[c], preferred_element_type=f32)
        for p in range(pre_n):
            part = product[p * hs : (p + 1) * hs]
            prod_f[c, p] = part
            prod_s[c, p] = part.astype(bf16)
        for d in range(1, pre_n):
            prod_copy(c, d).start()
        return carry

    lax.fori_loop(0, n_out, project, 0)
    for c in range(n_out):
        part = slice(c * out_width, (c + 1) * out_width)
        value = hid_ref[:, :, part].astype(f32).reshape(hs, out_width) + prod_f[c, pre]
        for d in range(1, pre_n):
            prod_copy(c, d).wait_recv()
            value = value + prod_r[c, d - 1].astype(f32)
        res_g[grp, pre, :, part] = value.astype(bf16)
        res_out[:, :, part] = value.reshape(hid_local, STEPS, out_width).astype(bf16)
    for d in range(1, pre_n):
        res_copy(d).start()
    for e in range(1, split):
        pass_copy(e, 0).start()
    for d in range(1, pre_n):
        res_copy(d).wait_recv()
        for e in range(1, split):
            pass_copy(e, d).start()

    spread_from = iota((LANES, 4 * LANES), 0)
    spread_to = iota((LANES, 4 * LANES), 1)
    spread = jnp.where(
        spread_to
        == jnp.where(spread_to < 2 * LANES, 2 * spread_from, 2 * LANES + 2 * spread_from + 1),
        1.0,
        0.0,
    ).astype(bf16)

    def spread_rows(e, residual):
        normed = (residual * gain_ref[...].astype(f32).reshape(1, depth)).astype(bf16)
        gate_rows = slice(e * everyone, (e + 1) * everyone)
        up_rows = slice((split + e) * everyone, (split + e + 1) * everyone)
        for j in range(depth // LANES):
            part = jnp.dot(
                normed[:, j * LANES : (j + 1) * LANES], spread, preferred_element_type=f32
            ).astype(bf16)
            x_exp[gate_rows, 2 * j * LANES : 2 * (j + 1) * LANES] = part[:, : 2 * LANES]
            x_exp[up_rows, 2 * j * LANES : 2 * (j + 1) * LANES] = part[:, 2 * LANES :]

    residual = res_g[grp].astype(f32).reshape(everyone, depth)
    squares = jnp.sum(residual * residual, axis=1, keepdims=True)
    for r in range(row_n):
        sq_s[r] = jnp.broadcast_to(squares[r * rs : (r + 1) * rs], (rs, LANES))
    for d in range(1, row_n):
        sq_copy(d).start()
    spread_rows(0, residual)
    for e in range(1, split):
        for d in range(pre_n):
            pass_copy(e, d).wait_recv()
    for e in range(1, split):
        spread_rows(e, res_g[across(e)].astype(f32).reshape(everyone, depth))

    tile_step = 2 if tiles_group % 2 == 0 else 1

    def gate_up_group(g, carry):
        for t in range(0, tiles_group, tile_step):
            tiles = [g * tiles_group + t + i for i in range(tile_step)]
            for tile in tiles:
                gu_copy(tile).wait()
            weights = [gu[tile].reshape(2 * depth, LANES) for tile in tiles]
            weight = jnp.concatenate(weights, axis=1) if tile_step > 1 else weights[0]
            product = jnp.dot(x_exp[...], weight, preferred_element_type=f32)
            part = slice(t * LANES, (t + tile_step) * LANES)
            for e in range(split):
                for r in range(row_n):
                    at = e * everyone + r * rs
                    up_at = split * everyone + at
                    both = jnp.concatenate(
                        [product[at : at + rs], product[up_at : up_at + rs]], axis=0
                    )
                    if e == 0:
                        gate_f[g, r, :, part] = both
                    gate_s[g, e, r, :, part] = both.astype(bf16)
        for e, d in others:
            gate_copy(g, e, d).start()
        return carry

    lax.fori_loop(0, FFN_GROUPS, gate_up_group, 0)

    square_sum = sq_s[row]
    for d in range(1, row_n):
        sq_copy(d).wait_recv()
        square_sum = square_sum + sq_r[d - 1]
    inverse = lax.rsqrt(square_sum[:, :1] / D + 1e-05)

    def activate(g, carry):
        for e in range(split):
            both = gate_f[g, row] if e == 0 else jnp.zeros((2 * rs, group_width), f32)
            for d in range(1 if e == 0 else 0, row_n):
                gate_copy(g, e, d).wait_recv()
                both = both + gate_r[g, e, d].astype(f32)
            gate = both[:rs] * inverse
            up = both[rs:] * inverse
            start = lax.rem(grp + split - e, split) * share + g * group_width
            part = pl.ds(pl.multiple_of(start, LANES), group_width)
            value = gate / (1.0 + jnp.exp(-gate)) * up * ffn8[:, part]
            act_out[:, :, part] = value.reshape(row_local, STEPS, group_width).astype(bf16)
        for e, d in others:
            gate_copy(g, e, d).wait_send()
        return carry

    lax.fori_loop(0, FFN_GROUPS, activate, 0)

    for d in range(1, pre_n):
        stat_copy(d).wait_send()
        acc_copy(d).wait_send()
        res_copy(d).wait_send()
        for c in range(n_out):
            prod_copy(c, d).wait_send()
    for e in range(1, split):
        for d in range(pre_n):
            pass_copy(e, d).wait_send()
    for d in range(1, row_n):
        mix_copy(d).wait_send()
        sq_copy(d).wait_send()


def hand_on(residual_ref, activation_ref, residual_out, activation_out):
    residual_out[...] = residual_ref[...]
    activation_out[...] = activation_ref[...]


def per_device(
    queries,
    prefix_keys,
    prefix_values,
    suffix_keys,
    suffix_values,
    new_keys,
    new_values,
    hidden,
    adapter_ids,
    suffix_lengths,
    kv_scales,
    ffn_scales,
    out_weight,
    norm_gain,
    gate_up,
):
    pre_n = lax.axis_size("pre")
    row_n = lax.axis_size("row")
    row_local = queries.shape[0]
    rs = row_local * STEPS
    hs = hidden.shape[0] * STEPS
    kv_width = prefix_keys.shape[1]
    adapters, ff = ffn_scales.shape
    block, cols = out_weight.shape
    depth = gate_up.shape[0]
    out_width = min(cols, 512)
    n_out = cols // out_width
    grp_n = lax.axis_size("grp")
    fits = ff % (grp_n * FFN_GROUPS * LANES) == 0
    split = grp_n if fits else 1
    n_tiles = ff // LANES // split
    group_width = ff // split // FFN_GROUPS
    everyone = row_n * rs
    dma = pltpu.SemaphoreType.DMA
    vmem = pl.BlockSpec(memory_space=pltpu.VMEM)
    smem = pl.BlockSpec(memory_space=pltpu.SMEM)
    hbm = pl.BlockSpec(memory_space=pl.ANY)
    scratch = [
        pltpu.VMEM((n_out, block, out_width), bf16),
        pltpu.VMEM((n_tiles, depth, 2, LANES), bf16),
        pltpu.VMEM((adapters, ff), bf16),
        pltpu.VMEM((rs, D), f32),
        pltpu.VMEM((rs, kv_width), f32),
        pltpu.VMEM((rs, kv_width), f32),
        pltpu.VMEM((rs, kv_width), f32),
        pltpu.VMEM((rs, kv_width), f32),
        pltpu.VMEM((pre_n, rs, block), bf16),
        pltpu.VMEM((pre_n - 1, rs, block), bf16),
        pltpu.VMEM((pre_n, 2, rs, LANES), f32),
        pltpu.VMEM((pre_n - 1, 2, rs, LANES), f32),
        pltpu.VMEM((row_n, rs, block), bf16),
        pltpu.VMEM((everyone, block), bf16),
        pltpu.VMEM((n_out, pre_n, hs, out_width), bf16),
        pltpu.VMEM((n_out, pre_n, hs, out_width), f32),
        pltpu.VMEM((n_out, pre_n - 1, hs, out_width), bf16),
        pltpu.VMEM((split, pre_n, hs, cols), bf16),
        pltpu.VMEM((2 * split * everyone, 2 * depth), bf16),
        pltpu.VMEM((FFN_GROUPS, split, row_n, 2 * rs, group_width), bf16),
        pltpu.VMEM((FFN_GROUPS, row_n, 2 * rs, group_width), f32),
        pltpu.VMEM((FFN_GROUPS, split, row_n, 2 * rs, group_width), bf16),
        pltpu.VMEM((row_n, rs, LANES), f32),
        pltpu.VMEM((row_n - 1, rs, LANES), f32),
        pltpu.VMEM((rs, ff), f32),
        dma((n_out,)),
        dma((n_tiles,)),
        dma,
        dma((2, pre_n - 1)),
        dma((2, pre_n - 1)),
        dma((2, row_n - 1)),
        dma((2, n_out, pre_n - 1)),
        dma((2, pre_n - 1)),
        dma((2, max(split - 1, 1), pre_n)),
        dma((2, FFN_GROUPS, split, row_n)),
        dma((2, row_n - 1)),
    ]
    outputs = pl.pallas_call(
        functools.partial(layer_kernel, (pre_n, row_n, split)),
        out_shape=(
            jax.ShapeDtypeStruct(hidden.shape, bf16),
            jax.ShapeDtypeStruct((row_local, STEPS, ff), bf16),
        ),
        in_specs=[smem, smem] + [vmem] * 10 + [hbm] * 3,
        out_specs=(vmem, vmem),
        scratch_shapes=scratch,
        compiler_params=pltpu.CompilerParams(
            collective_id=0, has_side_effects=True, vmem_limit_bytes=56 * 1024 * 1024
        ),
    )(
        adapter_ids,
        suffix_lengths,
        queries,
        prefix_keys,
        prefix_values,
        suffix_keys,
        suffix_values,
        new_keys,
        new_values,
        hidden,
        kv_scales,
        norm_gain,
        ffn_scales,
        out_weight,
        gate_up,
    )
    return pl.pallas_call(
        hand_on,
        out_shape=tuple(jax.ShapeDtypeStruct(value.shape, value.dtype) for value in outputs),
        in_specs=[vmem, vmem],
        out_specs=(vmem, vmem),
    )(*outputs)


def solution(mesh):
    placed = (
        P(("grp", "row"), None, None),
        P(("grp", "pre"), None),
        P(("grp", "pre"), None),
        P(("grp", "row"), "pre", None),
        P(("grp", "row"), "pre", None),
        P(("grp", "row"), None, None),
        P(("grp", "row"), None, None),
        P(("grp", "pre"), None, "row"),
        P(("grp", "row")),
        P(("grp", "row")),
        P(),
        P(None, "pre"),
        P("pre", "row"),
        P("row"),
        P("row", None, "pre"),
    )
    return jax.shard_map(
        per_device,
        mesh=mesh,
        in_specs=placed,
        out_specs=(P(("grp", "pre"), None, "row"), P(("grp", "row"), None, "pre")),
        check_vma=False,
    )
```

profile of v0, /device:TPU:0, one launch (start us, length us, event | category | flops | bytes accessed | tf_op | source)
XLA Modules:
  0.0 45.7 jit_solution(4095484189505329987)
XLA Ops:
  0.6 43.5 %shard_map.158 = (bf16[4,2,2048]{2,1,0:T(2,128)(2,1)}, bf16[4,2,3584]{2,1,0:T(2,128)(2,1)}) custom-call(s32[4]{0:T(128)} %ids_ref.1, s32[4]{0:T(128)} %lens_ref.1, bf16[4,2,8192]{2,1,0:T(2,128)(2,1)} %q_ref.1, bf16[128,1024]{1,0:T(8,128)(2,1)} %pk_ref.1, bf16[128,1024]{1,0:T(8,128)(2,1)} %pv_ref.1, bf16[4,16,1024]{2,1,0:T(8,128)(2,1)} %sk_ref.1, ...), custom_call_target="tpu_custom_call" | custom-call | tf_op jit(solution)/shard_map/pallas_call | solution.py:553
  44.2 1.5 %shard_map.159 = (bf16[4,2,2048]{2,1,0:T(2,128)(2,1)}, bf16[4,2,3584]{2,1,0:T(2,128)(2,1)}) custom-call(bf16[4,2,2048]{2,1,0:T(2,128)(2,1)} %get-tuple-element.4.residual_ref, bf16[4,2,3584]{2,1,0:T(2,128)(2,1)} %get-tuple-element.5.activation_ref), custom_call_target="tpu_custom_call" | custom-call | tf_op jit(solution)/shard_map/pallas_call | solution.py:582
where the time goes:
time: 45.9 us; the launch traced here: 45.7 us
  Pallas kernels  45 us (98%)
  between operations  0.64 us (1%)
    pallas_call x1, Pallas kernels, per_device(): pl.pallas_call(functools.partial(layer_kernel, (pre_n, row_n, split)), ou...  43.5 us
    pallas_call x1, Pallas kernels, per_device(): pl.pallas_call(hand_on, out_shape=tuple((jax.ShapeDtypeStruct(value.shape...  1.48 us

commit v1 on v0

--- a/solution.py
+++ b/solution.py
@@ -105,6 +105,8 @@
     tiles_group = n_tiles // FFN_GROUPS
     everyone = row_n * rs
 
+    gu_rows = gu_hbm.reshape(2 * depth, ff)
+
     def ow_copy(c):
         return pltpu.make_async_copy(
             ow_hbm.at[:, pl.ds(c * out_width, out_width)], ow.at[c], ow_sem.at[c]
@@ -112,7 +114,7 @@
 
     def gu_copy(c):
         return pltpu.make_async_copy(
-            gu_hbm.at[:, :, pl.ds(pl.multiple_of(grp * share + c * LANES, LANES), LANES)], gu.at[c], gu_sem.at[c]
+            gu_rows.at[:, pl.ds(pl.multiple_of(grp * share + c * LANES, LANES), LANES)], gu.at[c], gu_sem.at[c]
         )
 
     ffs_copy = pltpu.make_async_copy(ffs_hbm, ffs, ffs_sem)
@@ -313,12 +315,6 @@
 
         attend(ahead(d), finish)
 
-    ffs_copy.wait()
-    ffn_pick = jnp.where(
-        iota((rs, adapters), 1) == per_row(ids_ref, (rs, adapters)), 1.0, 0.0
-    ).astype(bf16)
-    ffn8[...] = jnp.dot(ffn_pick, ffs[...], preferred_element_type=f32)
-
     for d in range(1, pre_n):
         stat_copy(d).wait_recv()
     peak_of = [stat_s[pre, 0]] + [stat_r[d - 1, 0] for d in range(1, pre_n)]
@@ -366,6 +362,12 @@
         res_copy(d).start()
     for e in range(1, split):
         pass_copy(e, 0).start()
+    ffs_copy.wait()
+    ffn_pick = jnp.where(
+        iota((rs, adapters), 1) == per_row(ids_ref, (rs, adapters)), 1.0, 0.0
+    ).astype(bf16)
+    ffn8[...] = jnp.dot(ffn_pick, ffs[...], preferred_element_type=f32)
+
     for d in range(1, pre_n):
         res_copy(d).wait_recv()
         for e in range(1, split):
@@ -411,7 +413,7 @@
             tiles = [g * tiles_group + t + i for i in range(tile_step)]
             for tile in tiles:
                 gu_copy(tile).wait()
-            weights = [gu[tile].reshape(2 * depth, LANES) for tile in tiles]
+            weights = [gu[tile] for tile in tiles]
             weight = jnp.concatenate(weights, axis=1) if tile_step > 1 else weights[0]
             product = jnp.dot(x_exp[...], weight, preferred_element_type=f32)
             part = slice(t * LANES, (t + tile_step) * LANES)
@@ -514,7 +516,7 @@
     hbm = pl.BlockSpec(memory_space=pl.ANY)
     scratch = [
         pltpu.VMEM((n_out, block, out_width), bf16),
-        pltpu.VMEM((n_tiles, depth, 2, LANES), bf16),
+        pltpu.VMEM((n_tiles, 2 * depth, LANES), bf16),
         pltpu.VMEM((adapters, ff), bf16),
         pltpu.VMEM((rs, D), f32),
         pltpu.VMEM((rs, kv_width), f32),

time: 45.9 us -> 41.4 us (0.902)
  Pallas kernels: 45 us -> 40.6 us
    pallas_call x1, Pallas kernels: 43.5 us -> 39.1 us  [per_device(): pl.pallas_call(functools.partial(layer_kernel, (pre_n, row_n, split)), ou...]
where the time goes in v1:
time: 41.4 us; the launch traced here: 41.2 us
  Pallas kernels  40.6 us (98%)
  between operations  0.64 us (2%)
    pallas_call x1, Pallas kernels, per_device(): pl.pallas_call(functools.partial(layer_kernel, (pre_n, row_n, split)), ou...  39.1 us
    pallas_call x1, Pallas kernels, per_device(): pl.pallas_call(hand_on, out_shape=tuple((jax.ShapeDtypeStruct(value.shape...  1.48 us

profile of v1, /device:TPU:0, one launch (start us, length us, event | category | flops | bytes accessed | tf_op | source)
XLA Modules:
  0.0 41.2 jit_solution(2451188870310040834)
XLA Ops:
  0.6 39.1 %shard_map.158 = (bf16[4,2,2048]{2,1,0:T(2,128)(2,1)}, bf16[4,2,3584]{2,1,0:T(2,128)(2,1)}) custom-call(s32[4]{0:T(128)} %ids_ref.1, s32[4]{0:T(128)} %lens_ref.1, bf16[4,2,8192]{2,1,0:T(2,128)(2,1)} %q_ref.1, bf16[128,1024]{1,0:T(8,128)(2,1)} %pk_ref.1, bf16[128,1024]{1,0:T(8,128)(2,1)} %pv_ref.1, bf16[4,16,1024]{2,1,0:T(8,128)(2,1)} %sk_ref.1, ...), custom_call_target="tpu_custom_call" | custom-call | tf_op jit(solution)/shard_map/pallas_call | solution.py:555
  39.8 1.5 %shard_map.159 = (bf16[4,2,2048]{2,1,0:T(2,128)(2,1)}, bf16[4,2,3584]{2,1,0:T(2,128)(2,1)}) custom-call(bf16[4,2,2048]{2,1,0:T(2,128)(2,1)} %get-tuple-element.4.residual_ref, bf16[4,2,3584]{2,1,0:T(2,128)(2,1)} %get-tuple-element.5.activation_ref), custom_call_target="tpu_custom_call" | custom-call | tf_op jit(solution)/shard_map/pallas_call | solution.py:584

commit v2 on v1

--- a/solution.py
+++ b/solution.py
@@ -16,6 +16,8 @@
 LANES = 128
 FFN_GROUPS = 7
 
+GRANT = 40
+
 masked_score = -1e30
 f32 = jnp.float32
 bf16 = jnp.bfloat16
@@ -27,6 +29,23 @@
 
 def layer_kernel(
     sizes,
+    ids_hbm,
+    lens_hbm,
+    q_hbm,
+    pk_hbm,
+    pv_hbm,
+    sk_hbm,
+    sv_hbm,
+    nk_hbm,
+    nv_hbm,
+    hid_hbm,
+    kvs_hbm,
+    gain_hbm,
+    ffs_hbm,
+    ow_hbm,
+    gu_hbm,
+    res_out,
+    act_out,
     ids_ref,
     lens_ref,
     q_ref,
@@ -39,11 +58,6 @@
     hid_ref,
     kvs_ref,
     gain_ref,
-    ffs_hbm,
-    ow_hbm,
-    gu_hbm,
-    res_out,
-    act_out,
     ow,
     gu,
     ffs,
@@ -69,6 +83,7 @@
     sq_s,
     sq_r,
     ffn8,
+    in_sem,
     ow_sem,
     gu_sem,
     ffs_sem,
@@ -85,7 +100,7 @@
     grp = lax.rem(lax.axis_index("grp"), split)
     pre = lax.axis_index("pre")
     row = lax.axis_index("row")
-    row_local = q_ref.shape[0]
+    row_local = q_hbm.shape[0]
     rs = row_local * STEPS
     hid_local = hid_ref.shape[0]
     hs = hid_local * STEPS
@@ -117,6 +132,26 @@
             gu_rows.at[:, pl.ds(pl.multiple_of(grp * share + c * LANES, LANES), LANES)], gu.at[c], gu_sem.at[c]
         )
 
+    staged = [
+        (ids_hbm, ids_ref),
+        (lens_hbm, lens_ref),
+        (kvs_hbm, kvs_ref),
+        (q_hbm, q_ref),
+        (nk_hbm, nk_ref),
+        (nv_hbm, nv_ref),
+        (sk_hbm, sk_ref),
+        (pk_hbm, pk_ref),
+        (sv_hbm, sv_ref),
+        (pv_hbm, pv_ref),
+        (hid_hbm, hid_ref),
+        (gain_hbm, gain_ref),
+    ]
+    staged = [
+        pltpu.make_async_copy(source, target, in_sem.at[i])
+        for i, (source, target) in enumerate(staged)
+    ]
+    for copy in staged:
+        copy.start()
     ffs_copy = pltpu.make_async_copy(ffs_hbm, ffs, ffs_sem)
     for c in range(n_out):
         ow_copy(c).start()
@@ -214,6 +249,8 @@
             out = jnp.where(which == r, ref[r], out)
         return out
 
+    for copy in staged[:6]:
+        copy.wait()
     adapter = per_row(ids_ref, (rs, 2 * adapters))
     lane = iota((rs, 2 * adapters), 1)
     pick_key = jnp.where(lane == 2 * adapter, 1.0, 0.0)
@@ -304,6 +341,8 @@
         stat_s[b, 1] = totals
         finish()
 
+    for copy in staged[6:]:
+        copy.wait()
     for d in list(range(1, pre_n)) + [0]:
 
         def finish(d=d):
@@ -471,9 +510,13 @@
         sq_copy(d).wait_send()
 
 
-def hand_on(residual_ref, activation_ref, residual_out, activation_out):
-    residual_out[...] = residual_ref[...]
-    activation_out[...] = activation_ref[...]
+def hand_on(residual_ref, activation_ref, residual_out, activation_out, sem):
+    residual = pltpu.make_async_copy(residual_ref, residual_out, sem.at[0])
+    activation = pltpu.make_async_copy(activation_ref, activation_out, sem.at[1])
+    residual.start()
+    activation.start()
+    residual.wait()
+    activation.wait()
 
 
 def per_device(
@@ -512,9 +555,20 @@
     everyone = row_n * rs
     dma = pltpu.SemaphoreType.DMA
     vmem = pl.BlockSpec(memory_space=pltpu.VMEM)
-    smem = pl.BlockSpec(memory_space=pltpu.SMEM)
-    hbm = pl.BlockSpec(memory_space=pl.ANY)
+    hbm = pl.BlockSpec(memory_space=pltpu.HBM)
     scratch = [
+        pltpu.SMEM(adapter_ids.shape, jnp.int32),
+        pltpu.SMEM(suffix_lengths.shape, jnp.int32),
+        pltpu.VMEM(queries.shape, bf16),
+        pltpu.VMEM(prefix_keys.shape, bf16),
+        pltpu.VMEM(prefix_values.shape, bf16),
+        pltpu.VMEM(suffix_keys.shape, bf16),
+        pltpu.VMEM(suffix_values.shape, bf16),
+        pltpu.VMEM(new_keys.shape, bf16),
+        pltpu.VMEM(new_values.shape, bf16),
+        pltpu.VMEM(hidden.shape, bf16),
+        pltpu.VMEM(kv_scales.shape, bf16),
+        pltpu.VMEM(norm_gain.shape, bf16),
         pltpu.VMEM((n_out, block, out_width), bf16),
         pltpu.VMEM((n_tiles, 2 * depth, LANES), bf16),
         pltpu.VMEM((adapters, ff), bf16),
@@ -540,6 +594,7 @@
         pltpu.VMEM((row_n, rs, LANES), f32),
         pltpu.VMEM((row_n - 1, rs, LANES), f32),
         pltpu.VMEM((rs, ff), f32),
+        dma((12,)),
         dma((n_out,)),
         dma((n_tiles,)),
         dma,
@@ -558,34 +613,41 @@
             jax.ShapeDtypeStruct(hidden.shape, bf16),
             jax.ShapeDtypeStruct((row_local, STEPS, ff), bf16),
         ),
-        in_specs=[smem, smem] + [vmem] * 10 + [hbm] * 3,
+        in_specs=[hbm] * 15,
         out_specs=(vmem, vmem),
         scratch_shapes=scratch,
         compiler_params=pltpu.CompilerParams(
-            collective_id=0, has_side_effects=True, vmem_limit_bytes=56 * 1024 * 1024
+            collective_id=0, has_side_effects=True, vmem_limit_bytes=GRANT * 1024 * 1024
         ),
     )(
-        adapter_ids,
-        suffix_lengths,
-        queries,
-        prefix_keys,
-        prefix_values,
-        suffix_keys,
-        suffix_values,
-        new_keys,
-        new_values,
-        hidden,
-        kv_scales,
-        norm_gain,
-        ffn_scales,
-        out_weight,
-        gate_up,
+        *(
+            pltpu.with_memory_space_constraint(operand, pltpu.HBM)
+            for operand in (
+                adapter_ids,
+                suffix_lengths,
+                queries,
+                prefix_keys,
+                prefix_values,
+                suffix_keys,
+                suffix_values,
+                new_keys,
+                new_values,
+                hidden,
+                kv_scales,
+                norm_gain,
+                ffn_scales,
+                out_weight,
+                gate_up,
+            )
+        )
     )
     return pl.pallas_call(
         hand_on,
         out_shape=tuple(jax.ShapeDtypeStruct(value.shape, value.dtype) for value in outputs),
         in_specs=[vmem, vmem],
-        out_specs=(vmem, vmem),
+        out_specs=(hbm, hbm),
+        scratch_shapes=[dma((2,))],
+        compiler_params=pltpu.CompilerParams(vmem_limit_bytes=1024 * 1024),
     )(*outputs)
 
 

time: 41.4 us -> 44.2 us (1.068)
  Pallas kernels: 40.6 us -> 43.4 us
    pallas_call x1, Pallas kernels: 39.1 us -> 42.8 us  [per_device(): pl.pallas_call(functools.partial(layer_kernel, (pre_n, row_n, split)), ou...]
    pallas_call x1, Pallas kernels: 1.48 us -> 0.65 us  [per_device(): pl.pallas_call(hand_on, out_shape=tuple((jax.ShapeDtypeStruct(value.shape...]
where the time goes in v2:
time: 44.2 us; the launch traced here: 44.1 us
  Pallas kernels  43.4 us (98%)
  between operations  0.64 us (1%)
    pallas_call x1, Pallas kernels, per_device(): pl.pallas_call(functools.partial(layer_kernel, (pre_n, row_n, split)), ou...  42.8 us

profile of v2, /device:TPU:0, one launch (start us, length us, event | category | flops | bytes accessed | tf_op | source)
XLA Modules:
  0.0 44.1 jit_solution(16753454595049002164)
XLA Ops:
  0.6 42.8 %shard_map.158 = (bf16[4,2,2048]{2,1,0:T(2,128)(2,1)S(1)}, bf16[4,2,3584]{2,1,0:T(2,128)(2,1)S(1)}) custom-call(s32[4]{0:T(128)} %ids_hbm.1, s32[4]{0:T(128)} %lens_hbm.1, bf16[4,2,8192]{2,1,0:T(2,128)(2,1)} %q_hbm.1, bf16[128,1024]{1,0:T(8,128)(2,1)} %pk_hbm.1, bf16[128,1024]{1,0:T(8,128)(2,1)} %pv_hbm.1, bf16[4,16,1024]{2,1,0:T(8,128)(2,1)} %sk_hbm.1, ...), custom_call_target="tpu_custom_call" | custom-call | tf_op jit(solution)/shard_map/pallas_call | solution.py:610
  43.4 0.7 %shard_map.159 = (bf16[4,2,2048]{2,1,0:T(2,128)(2,1)}, bf16[4,2,3584]{2,1,0:T(2,128)(2,1)}) custom-call(bf16[4,2,2048]{2,1,0:T(2,128)(2,1)S(1)} %get-tuple-element.4.residual_ref, bf16[4,2,3584]{2,1,0:T(2,128)(2,1)S(1)} %get-tuple-element.5.activation_ref), custom_call_target="tpu_custom_call" | custom-call | tf_op jit(solution)/shard_map/pallas_call | solution.py:644

commit v3 on v2

--- a/solution.py
+++ b/solution.py
@@ -124,12 +124,12 @@
 
     def ow_copy(c):
         return pltpu.make_async_copy(
-            ow_hbm.at[:, pl.ds(c * out_width, out_width)], ow.at[c], ow_sem.at[c]
+            ow_hbm.at[:, pl.ds(c * out_width, out_width)], ow.at[c], ow_sem
         )
 
     def gu_copy(c):
         return pltpu.make_async_copy(
-            gu_rows.at[:, pl.ds(pl.multiple_of(grp * share + c * LANES, LANES), LANES)], gu.at[c], gu_sem.at[c]
+            gu_rows.at[:, pl.ds(pl.multiple_of(grp * share + c * LANES, LANES), LANES)], gu.at[c], gu_sem
         )
 
     staged = [
@@ -153,11 +153,9 @@
     for copy in staged:
         copy.start()
     ffs_copy = pltpu.make_async_copy(ffs_hbm, ffs, ffs_sem)
-    for c in range(n_out):
-        ow_copy(c).start()
-    ffs_copy.start()
-    for c in range(n_tiles):
-        gu_copy(c).start()
+
+    def landed(ref, sem):
+        pltpu.make_async_copy(ref, ref, sem).wait()
 
     barrier = pltpu.get_barrier_semaphore()
     for d in range(1, pre_n):
@@ -193,8 +191,8 @@
             device_id_type=pl.DeviceIdType.MESH,
         )
 
-    def pair(sem, *at):
-        return sem.at[(0,) + at], sem.at[(1,) + at]
+    def pair(sem, at=0):
+        return sem.at[0], sem.at[1 + at]
 
     def ahead(d):
         return lax.rem(pre + d, pre_n)
@@ -203,17 +201,17 @@
         return lax.rem(row + d, row_n)
 
     def acc_copy(d):
-        return remote(acc_s.at[ahead(d)], acc_r.at[d - 1], pair(acc_sem, d - 1), "pre", ahead(d))
+        return remote(acc_s.at[ahead(d)], acc_r.at[d - 1], pair(acc_sem), "pre", ahead(d))
 
     def stat_copy(d):
-        return remote(stat_s.at[ahead(d)], stat_r.at[d - 1], pair(stat_sem, d - 1), "pre", ahead(d))
+        return remote(stat_s.at[ahead(d)], stat_r.at[d - 1], pair(stat_sem), "pre", ahead(d))
 
     def mix_copy(d):
-        return remote(mix_g.at[row], mix_g.at[row], pair(mix_sem, d - 1), "row", beside(d))
+        return remote(mix_g.at[row], mix_g.at[row], pair(mix_sem), "row", beside(d))
 
     def prod_copy(c, d):
         return remote(
-            prod_s.at[c, ahead(d)], prod_r.at[c, d - 1], pair(prod_sem, c, d - 1), "pre", ahead(d)
+            prod_s.at[c, ahead(d)], prod_r.at[c, d - 1], pair(prod_sem, c), "pre", ahead(d)
         )
 
     def res_copy(d):
@@ -225,16 +223,16 @@
 
     def pass_copy(e, d):
         block_at = res_g.at[grp, lax.rem(pre + pre_n - d, pre_n)]
-        return remote(block_at, block_at, pair(pass_sem, e - 1, d), "grp", across(e))
+        return remote(block_at, block_at, pair(pass_sem), "grp", across(e))
 
     def sq_copy(d):
-        return remote(sq_s.at[beside(d)], sq_r.at[d - 1], pair(sq_sem, d - 1), "row", beside(d))
+        return remote(sq_s.at[beside(d)], sq_r.at[d - 1], pair(sq_sem), "row", beside(d))
 
     def gate_copy(g, e, d):
         return remote(
             gate_s.at[g, e, beside(d)],
-            gate_r.at[g, e, d],
-            pair(gate_sem, g, e, d),
+            gate_r.at[g, e * row_n + d - 1],
+            pair(gate_sem, g),
             "row",
             beside(d),
             across(e) if e > 0 else None,
@@ -249,8 +247,10 @@
             out = jnp.where(which == r, ref[r], out)
         return out
 
-    for copy in staged[:6]:
+    for copy in staged:
         copy.wait()
+    for c in range(n_out):
+        ow_copy(c).start()
     adapter = per_row(ids_ref, (rs, 2 * adapters))
     lane = iota((rs, 2 * adapters), 1)
     pick_key = jnp.where(lane == 2 * adapter, 1.0, 0.0)
@@ -341,29 +341,34 @@
         stat_s[b, 1] = totals
         finish()
 
-    for copy in staged[6:]:
-        copy.wait()
-    for d in list(range(1, pre_n)) + [0]:
-
-        def finish(d=d):
-            if d == 1:
+    def farthest(k):
+        down = jnp.where(pre_n - 1 - k > pre, pre_n - 1 - k, pre_n - 2 - k)
+        up = jnp.where(k < pre, k, k + 1)
+        target = jnp.where(2 * pre < pre_n, down, up)
+        return lax.rem(target - pre + pre_n, pre_n)
+
+    for k in range(pre_n):
+
+        def finish(k=k):
+            if k == 0:
                 pl.semaphore_wait(barrier, pre_n + row_n - 2 + (split - 1) * row_n)
-            if d > 0:
-                stat_copy(d).start()
-                acc_copy(d).start()
-
-        attend(ahead(d), finish)
-
-    for d in range(1, pre_n):
-        stat_copy(d).wait_recv()
+            if k < pre_n - 1:
+                stat_copy(farthest(k)).start()
+                acc_copy(farthest(k)).start()
+
+        attend(ahead(farthest(k)) if k < pre_n - 1 else pre, finish)
+
+    ffs_copy.start()
+    for c in range(n_tiles):
+        gu_copy(c).start()
+    landed(stat_r, stat_sem.at[1])
     peak_of = [stat_s[pre, 0]] + [stat_r[d - 1, 0] for d in range(1, pre_n)]
     total_of = [stat_s[pre, 1]] + [stat_r[d - 1, 1] for d in range(1, pre_n)]
     highest = functools.reduce(jnp.maximum, peak_of)
     factor_of = [jnp.exp(peak - highest) for peak in peak_of]
     weight_sum = sum(factor * total for factor, total in zip(factor_of, total_of))
     factor_of = [factor / weight_sum for factor in factor_of]
-    for d in range(1, pre_n):
-        acc_copy(d).wait_recv()
+    landed(acc_r, acc_sem.at[1])
     for j in range(heads_block):
         part = slice(j * HD, (j + 1) * HD)
         value = acc_s[pre, :, part].astype(f32) * factor_of[0][:, j : j + 1]
@@ -372,10 +377,8 @@
         mix_g[row, :, part] = value.astype(bf16)
     for d in range(1, row_n):
         mix_copy(d).start()
-    for c in range(n_out):
-        ow_copy(c).wait()
-    for d in range(1, row_n):
-        mix_copy(d).wait_recv()
+    landed(ow, ow_sem)
+    landed(mix_g.at[pl.ds(0, row_n - 1)], mix_sem.at[1])
     mix_x[...] = mix_g[...].astype(f32).reshape(everyone, block).astype(bf16)
 
     def project(c, carry):
@@ -392,8 +395,8 @@
     for c in range(n_out):
         part = slice(c * out_width, (c + 1) * out_width)
         value = hid_ref[:, :, part].astype(f32).reshape(hs, out_width) + prod_f[c, pre]
+        landed(prod_r.at[c], prod_sem.at[1 + c])
         for d in range(1, pre_n):
-            prod_copy(c, d).wait_recv()
             value = value + prod_r[c, d - 1].astype(f32)
         res_g[grp, pre, :, part] = value.astype(bf16)
         res_out[:, :, part] = value.reshape(hid_local, STEPS, out_width).astype(bf16)
@@ -439,19 +442,17 @@
     for d in range(1, row_n):
         sq_copy(d).start()
     spread_rows(0, residual)
-    for e in range(1, split):
-        for d in range(pre_n):
-            pass_copy(e, d).wait_recv()
+    if split > 1:
+        landed(res_g.at[pl.ds(0, split - 1)], pass_sem.at[1])
     for e in range(1, split):
         spread_rows(e, res_g[across(e)].astype(f32).reshape(everyone, depth))
 
+    landed(gu, gu_sem)
     tile_step = 2 if tiles_group % 2 == 0 else 1
 
     def gate_up_group(g, carry):
         for t in range(0, tiles_group, tile_step):
             tiles = [g * tiles_group + t + i for i in range(tile_step)]
-            for tile in tiles:
-                gu_copy(tile).wait()
             weights = [gu[tile] for tile in tiles]
             weight = jnp.concatenate(weights, axis=1) if tile_step > 1 else weights[0]
             product = jnp.dot(x_exp[...], weight, preferred_element_type=f32)
@@ -473,41 +474,36 @@
     lax.fori_loop(0, FFN_GROUPS, gate_up_group, 0)
 
     square_sum = sq_s[row]
+    landed(sq_r, sq_sem.at[1])
     for d in range(1, row_n):
-        sq_copy(d).wait_recv()
         square_sum = square_sum + sq_r[d - 1]
     inverse = lax.rsqrt(square_sum[:, :1] / D + 1e-05)
 
     def activate(g, carry):
+        landed(gate_r.at[g], gate_sem.at[1 + g])
         for e in range(split):
             both = gate_f[g, row] if e == 0 else jnp.zeros((2 * rs, group_width), f32)
             for d in range(1 if e == 0 else 0, row_n):
-                gate_copy(g, e, d).wait_recv()
-                both = both + gate_r[g, e, d].astype(f32)
+                both = both + gate_r[g, e * row_n + d - 1].astype(f32)
             gate = both[:rs] * inverse
             up = both[rs:] * inverse
             start = lax.rem(grp + split - e, split) * share + g * group_width
             part = pl.ds(pl.multiple_of(start, LANES), group_width)
             value = gate / (1.0 + jnp.exp(-gate)) * up * ffn8[:, part]
             act_out[:, :, part] = value.reshape(row_local, STEPS, group_width).astype(bf16)
-        for e, d in others:
-            gate_copy(g, e, d).wait_send()
         return carry
 
     lax.fori_loop(0, FFN_GROUPS, activate, 0)
 
-    for d in range(1, pre_n):
-        stat_copy(d).wait_send()
-        acc_copy(d).wait_send()
-        res_copy(d).wait_send()
-        for c in range(n_out):
-            prod_copy(c, d).wait_send()
-    for e in range(1, split):
-        for d in range(pre_n):
-            pass_copy(e, d).wait_send()
-    for d in range(1, row_n):
-        mix_copy(d).wait_send()
-        sq_copy(d).wait_send()
+    landed(stat_r, stat_sem.at[0])
+    landed(acc_r, acc_sem.at[0])
+    landed(mix_g.at[pl.ds(0, row_n - 1)], mix_sem.at[0])
+    landed(prod_r, prod_sem.at[0])
+    landed(res_g.at[0, pl.ds(0, pre_n - 1)], res_sem.at[0])
+    if split > 1:
+        landed(res_g.at[pl.ds(0, split - 1)], pass_sem.at[0])
+    landed(sq_r, sq_sem.at[0])
+    landed(gate_r, gate_sem.at[0])
 
 
 def hand_on(residual_ref, activation_ref, residual_out, activation_out, sem):
@@ -590,22 +586,22 @@
         pltpu.VMEM((2 * split * everyone, 2 * depth), bf16),
         pltpu.VMEM((FFN_GROUPS, split, row_n, 2 * rs, group_width), bf16),
         pltpu.VMEM((FFN_GROUPS, row_n, 2 * rs, group_width), f32),
-        pltpu.VMEM((FFN_GROUPS, split, row_n, 2 * rs, group_width), bf16),
+        pltpu.VMEM((FFN_GROUPS, split * row_n - 1, 2 * rs, group_width), bf16),
         pltpu.VMEM((row_n, rs, LANES), f32),
         pltpu.VMEM((row_n - 1, rs, LANES), f32),
         pltpu.VMEM((rs, ff), f32),
         dma((12,)),
-        dma((n_out,)),
-        dma((n_tiles,)),
         dma,
-        dma((2, pre_n - 1)),
-        dma((2, pre_n - 1)),
-        dma((2, row_n - 1)),
-        dma((2, n_out, pre_n - 1)),
-        dma((2, pre_n - 1)),
-        dma((2, max(split - 1, 1), pre_n)),
-        dma((2, FFN_GROUPS, split, row_n)),
-        dma((2, row_n - 1)),
+        dma,
+        dma,
+        dma((2,)),
+        dma((2,)),
+        dma((2,)),
+        dma((1 + n_out,)),
+        dma((pre_n,)),
+        dma((2,)),
+        dma((1 + FFN_GROUPS,)),
+        dma((2,)),
     ]
     outputs = pl.pallas_call(
         functools.partial(layer_kernel, (pre_n, row_n, split)),

time: 44.2 us -> 36.7 us (0.83)
  Pallas kernels: 43.4 us -> 35.9 us
    pallas_call x1, Pallas kernels: 42.8 us -> 35.2 us  [per_device(): pl.pallas_call(functools.partial(layer_kernel, (pre_n, row_n, split)), ou...]
where the time goes in v3:
time: 36.7 us; the launch traced here: 36.5 us
  Pallas kernels  35.9 us (98%)
  between operations  0.64 us (2%)
    pallas_call x1, Pallas kernels, per_device(): pl.pallas_call(functools.partial(layer_kernel, (pre_n, row_n, split)), ou...  35.2 us

profile of v3, /device:TPU:0, one launch (start us, length us, event | category | flops | bytes accessed | tf_op | source)
XLA Modules:
  0.0 36.5 jit_solution(17982094433378226984)
XLA Ops:
  0.6 35.2 %shard_map.158 = (bf16[4,2,2048]{2,1,0:T(2,128)(2,1)S(1)}, bf16[4,2,3584]{2,1,0:T(2,128)(2,1)S(1)}) custom-call(s32[4]{0:T(128)} %ids_hbm.1, s32[4]{0:T(128)} %lens_hbm.1, bf16[4,2,8192]{2,1,0:T(2,128)(2,1)} %q_hbm.1, bf16[128,1024]{1,0:T(8,128)(2,1)} %pk_hbm.1, bf16[128,1024]{1,0:T(8,128)(2,1)} %pv_hbm.1, bf16[4,16,1024]{2,1,0:T(8,128)(2,1)} %sk_hbm.1, ...), custom_call_target="tpu_custom_call" | custom-call | tf_op jit(solution)/shard_map/pallas_call | solution.py:606
  35.9 0.7 %shard_map.159 = (bf16[4,2,2048]{2,1,0:T(2,128)(2,1)}, bf16[4,2,3584]{2,1,0:T(2,128)(2,1)}) custom-call(bf16[4,2,2048]{2,1,0:T(2,128)(2,1)S(1)} %get-tuple-element.4.residual_ref, bf16[4,2,3584]{2,1,0:T(2,128)(2,1)S(1)} %get-tuple-element.5.activation_ref), custom_call_target="tpu_custom_call" | custom-call | tf_op jit(solution)/shard_map/pallas_call | solution.py:640

commit v4 on v3

--- a/solution.py
+++ b/solution.py
@@ -14,7 +14,7 @@
 STEPS = 2
 GROUP = HEADS // KV_HEADS
 LANES = 128
-FFN_GROUPS = 7
+OWN_SHARE = 0.4
 
 GRANT = 40
 
@@ -80,6 +80,7 @@
     gate_s,
     gate_f,
     gate_r,
+    gate_b,
     sq_s,
     sq_r,
     ffn8,
@@ -94,10 +95,11 @@
     res_sem,
     pass_sem,
     gate_sem,
+    both_sem,
     sq_sem,
 ):
-    pre_n, row_n, split = sizes
-    grp = lax.rem(lax.axis_index("grp"), split)
+    pre_n, row_n, split, own, shared = sizes
+    grp = lax.axis_index("grp")
     pre = lax.axis_index("pre")
     row = lax.axis_index("row")
     row_local = q_hbm.shape[0]
@@ -115,9 +117,8 @@
     score_scale = HD ** (-0.5)
     n_out, _, out_width = ow.shape
     n_tiles = gu.shape[0]
-    share = n_tiles * LANES
-    group_width = gate_s.shape[4]
-    tiles_group = n_tiles // FFN_GROUPS
+    unit = gate_s.shape[3]
+    unit_tiles = unit // LANES
     everyone = row_n * rs
 
     gu_rows = gu_hbm.reshape(2 * depth, ff)
@@ -129,8 +130,15 @@
 
     def gu_copy(c):
         return pltpu.make_async_copy(
-            gu_rows.at[:, pl.ds(pl.multiple_of(grp * share + c * LANES, LANES), LANES)], gu.at[c], gu_sem
-        )
+            gu_rows.at[:, pl.ds(start(c // unit_tiles) + c % unit_tiles * LANES, LANES)],
+            gu.at[c],
+            gu_sem,
+        )
+
+    def start(slot):
+        if slot < own:
+            return slot * unit
+        return pl.multiple_of((own + grp * shared + slot - own) * unit, LANES)
 
     staged = [
         (ids_hbm, ids_ref),
@@ -214,25 +222,31 @@
             prod_s.at[c, ahead(d)], prod_r.at[c, d - 1], pair(prod_sem, c), "pre", ahead(d)
         )
 
-    def res_copy(d):
-        block_at = res_g.at[grp, pre]
-        return remote(block_at, block_at, pair(res_sem, d - 1), "pre", ahead(d))
+    def res_copy(c, d):
+        block_at = res_g.at[grp, pre, :, pl.ds(c * out_width, out_width)]
+        return remote(block_at, block_at, pair(res_sem, c * (pre_n - 1) + d - 1), "pre", ahead(d))
 
     def across(e):
         return lax.rem(grp + e, split)
 
-    def pass_copy(e, d):
-        block_at = res_g.at[grp, lax.rem(pre + pre_n - d, pre_n)]
+    def pass_copy(c, e, d):
+        source = lax.rem(pre + pre_n - d, pre_n)
+        block_at = res_g.at[grp, source, :, pl.ds(c * out_width, out_width)]
         return remote(block_at, block_at, pair(pass_sem), "grp", across(e))
 
     def sq_copy(d):
         return remote(sq_s.at[beside(d)], sq_r.at[d - 1], pair(sq_sem), "row", beside(d))
 
-    def gate_copy(g, e, d):
+    def gate_copy(g, d):
         return remote(
-            gate_s.at[g, e, beside(d)],
-            gate_r.at[g, e * row_n + d - 1],
-            pair(gate_sem, g),
+            gate_s.at[g, beside(d)], gate_r.at[g, d - 1], pair(gate_sem, g), "row", beside(d)
+        )
+
+    def both_copy(i, e, d):
+        return remote(
+            gate_s.at[own + i * split + e, beside(d)],
+            gate_b.at[i, e * row_n + d - 1],
+            pair(both_sem, i),
             "row",
             beside(d),
             across(e) if e > 0 else None,
@@ -399,21 +413,22 @@
         for d in range(1, pre_n):
             value = value + prod_r[c, d - 1].astype(f32)
         res_g[grp, pre, :, part] = value.astype(bf16)
+        for d in range(1, pre_n):
+            res_copy(c, d).start()
+        for e in range(1, split):
+            pass_copy(c, e, 0).start()
         res_out[:, :, part] = value.reshape(hid_local, STEPS, out_width).astype(bf16)
-    for d in range(1, pre_n):
-        res_copy(d).start()
-    for e in range(1, split):
-        pass_copy(e, 0).start()
     ffs_copy.wait()
     ffn_pick = jnp.where(
         iota((rs, adapters), 1) == per_row(ids_ref, (rs, adapters)), 1.0, 0.0
     ).astype(bf16)
     ffn8[...] = jnp.dot(ffn_pick, ffs[...], preferred_element_type=f32)
 
-    for d in range(1, pre_n):
-        res_copy(d).wait_recv()
-        for e in range(1, split):
-            pass_copy(e, d).start()
+    for c in range(n_out):
+        for d in range(1, pre_n):
+            res_copy(c, d).wait_recv()
+            for e in range(1, split):
+                pass_copy(c, e, d).start()
 
     spread_from = iota((LANES, 4 * LANES), 0)
     spread_to = iota((LANES, 4 * LANES), 1)
@@ -426,14 +441,21 @@
 
     def spread_rows(e, residual):
         normed = (residual * gain_ref[...].astype(f32).reshape(1, depth)).astype(bf16)
-        gate_rows = slice(e * everyone, (e + 1) * everyone)
-        up_rows = slice((split + e) * everyone, (split + e + 1) * everyone)
-        for j in range(depth // LANES):
-            part = jnp.dot(
-                normed[:, j * LANES : (j + 1) * LANES], spread, preferred_element_type=f32
-            ).astype(bf16)
-            x_exp[gate_rows, 2 * j * LANES : 2 * (j + 1) * LANES] = part[:, : 2 * LANES]
-            x_exp[up_rows, 2 * j * LANES : 2 * (j + 1) * LANES] = part[:, 2 * LANES :]
+        first = 2 * e * everyone
+        gate_rows = slice(first, first + everyone)
+        up_rows = slice(first + everyone, first + 2 * everyone)
+        blocks = depth // LANES
+        batch = min(blocks, 4)
+        for j in range(0, blocks, batch):
+            stacked = jnp.concatenate(
+                [normed[:, k * LANES : (k + 1) * LANES] for k in range(j, j + batch)], axis=0
+            )
+            parts = jnp.dot(stacked, spread, preferred_element_type=f32).astype(bf16)
+            for k in range(batch):
+                part = parts[k * everyone : (k + 1) * everyone]
+                at = slice(2 * (j + k) * LANES, 2 * (j + k + 1) * LANES)
+                x_exp[gate_rows, at] = part[:, : 2 * LANES]
+                x_exp[up_rows, at] = part[:, 2 * LANES :]
 
     residual = res_g[grp].astype(f32).reshape(everyone, depth)
     squares = jnp.sum(residual * residual, axis=1, keepdims=True)
@@ -442,36 +464,45 @@
     for d in range(1, row_n):
         sq_copy(d).start()
     spread_rows(0, residual)
+    def unit_product(g, rows):
+        weights = [gu[g * unit_tiles + t] for t in range(unit_tiles)]
+        weight = jnp.concatenate(weights, axis=1) if unit_tiles > 1 else weights[0]
+        return jnp.dot(x_exp[:rows], weight, preferred_element_type=f32)
+
+    def gate_and_up(product, e, r):
+        at = 2 * e * everyone + r * rs
+        up_at = at + everyone
+        return jnp.concatenate([product[at : at + rs], product[up_at : up_at + rs]], axis=0)
+
+    def own_unit(g, carry):
+        product = unit_product(g, 2 * everyone)
+        for r in range(row_n):
+            both = gate_and_up(product, 0, r)
+            gate_f[g, r] = both
+            gate_s[g, r] = both.astype(bf16)
+        for d in range(1, row_n):
+            gate_copy(g, d).start()
+        return carry
+
+    def shared_unit(i, carry):
+        product = unit_product(own + i, 2 * split * everyone)
+        for e in range(split):
+            for r in range(row_n):
+                both = gate_and_up(product, e, r)
+                if e == 0:
+                    gate_f[own + i, r] = both
+                gate_s[own + i * split + e, r] = both.astype(bf16)
+        for e, d in others:
+            both_copy(i, e, d).start()
+        return carry
+
+    landed(gu, gu_sem)
+    lax.fori_loop(0, own, own_unit, 0)
     if split > 1:
         landed(res_g.at[pl.ds(0, split - 1)], pass_sem.at[1])
     for e in range(1, split):
         spread_rows(e, res_g[across(e)].astype(f32).reshape(everyone, depth))
-
-    landed(gu, gu_sem)
-    tile_step = 2 if tiles_group % 2 == 0 else 1
-
-    def gate_up_group(g, carry):
-        for t in range(0, tiles_group, tile_step):
-            tiles = [g * tiles_group + t + i for i in range(tile_step)]
-            weights = [gu[tile] for tile in tiles]
-            weight = jnp.concatenate(weights, axis=1) if tile_step > 1 else weights[0]
-            product = jnp.dot(x_exp[...], weight, preferred_element_type=f32)
-            part = slice(t * LANES, (t + tile_step) * LANES)
-            for e in range(split):
-                for r in range(row_n):
-                    at = e * everyone + r * rs
-                    up_at = split * everyone + at
-                    both = jnp.concatenate(
-                        [product[at : at + rs], product[up_at : up_at + rs]], axis=0
-                    )
-                    if e == 0:
-                        gate_f[g, r, :, part] = both
-                    gate_s[g, e, r, :, part] = both.astype(bf16)
-        for e, d in others:
-            gate_copy(g, e, d).start()
-        return carry
-
-    lax.fori_loop(0, FFN_GROUPS, gate_up_group, 0)
+    lax.fori_loop(0, shared, shared_unit, 0)
 
     square_sum = sq_s[row]
     landed(sq_r, sq_sem.at[1])
@@ -479,21 +510,33 @@
         square_sum = square_sum + sq_r[d - 1]
     inverse = lax.rsqrt(square_sum[:, :1] / D + 1e-05)
 
-    def activate(g, carry):
+    def activate(both, at):
+        gate = both[:rs] * inverse
+        up = both[rs:] * inverse
+        part = pl.ds(pl.multiple_of(at, LANES), unit)
+        value = gate / (1.0 + jnp.exp(-gate)) * up * ffn8[:, part]
+        act_out[:, :, part] = value.reshape(row_local, STEPS, unit).astype(bf16)
+
+    def finish_own(g, carry):
         landed(gate_r.at[g], gate_sem.at[1 + g])
+        both = gate_f[g, row]
+        for d in range(1, row_n):
+            both = both + gate_r[g, d - 1].astype(f32)
+        activate(both, g * unit)
+        return carry
+
+    def finish_shared(i, carry):
+        landed(gate_b.at[i], both_sem.at[1 + i])
         for e in range(split):
-            both = gate_f[g, row] if e == 0 else jnp.zeros((2 * rs, group_width), f32)
+            both = gate_f[own + i, row] if e == 0 else jnp.zeros((2 * rs, unit), f32)
             for d in range(1 if e == 0 else 0, row_n):
-                both = both + gate_r[g, e * row_n + d - 1].astype(f32)
-            gate = both[:rs] * inverse
-            up = both[rs:] * inverse
-            start = lax.rem(grp + split - e, split) * share + g * group_width
-            part = pl.ds(pl.multiple_of(start, LANES), group_width)
-            value = gate / (1.0 + jnp.exp(-gate)) * up * ffn8[:, part]
-            act_out[:, :, part] = value.reshape(row_local, STEPS, group_width).astype(bf16)
+                both = both + gate_b[i, e * row_n + d - 1].astype(f32)
+            owner = lax.rem(grp + split - e, split)
+            activate(both, (own + owner * shared + i) * unit)
         return carry
 
-    lax.fori_loop(0, FFN_GROUPS, activate, 0)
+    lax.fori_loop(0, own, finish_own, 0)
+    lax.fori_loop(0, shared, finish_shared, 0)
 
     landed(stat_r, stat_sem.at[0])
     landed(acc_r, acc_sem.at[0])
@@ -504,6 +547,7 @@
         landed(res_g.at[pl.ds(0, split - 1)], pass_sem.at[0])
     landed(sq_r, sq_sem.at[0])
     landed(gate_r, gate_sem.at[0])
+    landed(gate_b, both_sem.at[0])
 
 
 def hand_on(residual_ref, activation_ref, residual_out, activation_out, sem):
@@ -543,11 +587,12 @@
     depth = gate_up.shape[0]
     out_width = min(cols, 512)
     n_out = cols // out_width
-    grp_n = lax.axis_size("grp")
-    fits = ff % (grp_n * FFN_GROUPS * LANES) == 0
-    split = grp_n if fits else 1
-    n_tiles = ff // LANES // split
-    group_width = ff // split // FFN_GROUPS
+    split = lax.axis_size("grp")
+    unit = 2 * LANES if ff % (2 * LANES) == 0 else LANES
+    units = ff // unit
+    shared = int(units * (1 - OWN_SHARE)) // split
+    own = units - shared * split
+    n_tiles = (own + shared) * unit // LANES
     everyone = row_n * rs
     dma = pltpu.SemaphoreType.DMA
     vmem = pl.BlockSpec(memory_space=pltpu.VMEM)
@@ -584,9 +629,10 @@
         pltpu.VMEM((n_out, pre_n - 1, hs, out_width), bf16),
         pltpu.VMEM((split, pre_n, hs, cols), bf16),
         pltpu.VMEM((2 * split * everyone, 2 * depth), bf16),
-        pltpu.VMEM((FFN_GROUPS, split, row_n, 2 * rs, group_width), bf16),
-        pltpu.VMEM((FFN_GROUPS, row_n, 2 * rs, group_width), f32),
-        pltpu.VMEM((FFN_GROUPS, split * row_n - 1, 2 * rs, group_width), bf16),
+        pltpu.VMEM((own + shared * split, row_n, 2 * rs, unit), bf16),
+        pltpu.VMEM((own + shared, row_n, 2 * rs, unit), f32),
+        pltpu.VMEM((own, row_n - 1, 2 * rs, unit), bf16),
+        pltpu.VMEM((shared, split * row_n - 1, 2 * rs, unit), bf16),
         pltpu.VMEM((row_n, rs, LANES), f32),
         pltpu.VMEM((row_n - 1, rs, LANES), f32),
         pltpu.VMEM((rs, ff), f32),
@@ -598,13 +644,14 @@
         dma((2,)),
         dma((2,)),
         dma((1 + n_out,)),
-        dma((pre_n,)),
+        dma((1 + n_out * (pre_n - 1),)),
         dma((2,)),
-        dma((1 + FFN_GROUPS,)),
+        dma((1 + own,)),
+        dma((1 + shared,)),
         dma((2,)),
     ]
     outputs = pl.pallas_call(
-        functools.partial(layer_kernel, (pre_n, row_n, split)),
+        functools.partial(layer_kernel, (pre_n, row_n, split, own, shared)),
         out_shape=(
             jax.ShapeDtypeStruct(hidden.shape, bf16),
             jax.ShapeDtypeStruct((row_local, STEPS, ff), bf16),

time: 36.7 us -> 34.2 us (0.932)
  Pallas kernels: 35.9 us -> 33.4 us
    pallas_call x1, Pallas kernels: 35.2 us -> 32.7 us  [per_device(): pl.pallas_call(functools.partial(layer_kernel, (pre_n, row_n, split, own,...]
where the time goes in v4:
time: 34.2 us; the launch traced here: 34 us
  Pallas kernels  33.4 us (98%)
  between operations  0.64 us (2%)
    pallas_call x1, Pallas kernels, per_device(): pl.pallas_call(functools.partial(layer_kernel, (pre_n, row_n, split, own,...  32.7 us

profile of v4, /device:TPU:0, one launch (start us, length us, event | category | flops | bytes accessed | tf_op | source)
XLA Modules:
  0.0 34.0 jit_solution(1498336216505969538)
XLA Ops:
  0.6 32.7 %shard_map.158 = (bf16[4,2,2048]{2,1,0:T(2,128)(2,1)S(1)}, bf16[4,2,3584]{2,1,0:T(2,128)(2,1)S(1)}) custom-call(s32[4]{0:T(128)} %ids_hbm.1, s32[4]{0:T(128)} %lens_hbm.1, bf16[4,2,8192]{2,1,0:T(2,128)(2,1)} %q_hbm.1, bf16[128,1024]{1,0:T(8,128)(2,1)} %pk_hbm.1, bf16[128,1024]{1,0:T(8,128)(2,1)} %pv_hbm.1, bf16[4,16,1024]{2,1,0:T(8,128)(2,1)} %sk_hbm.1, ...), custom_call_target="tpu_custom_call" | custom-call | tf_op jit(solution)/shard_map/pallas_call | solution.py:653
  33.4 0.7 %shard_map.159 = (bf16[4,2,2048]{2,1,0:T(2,128)(2,1)}, bf16[4,2,3584]{2,1,0:T(2,128)(2,1)}) custom-call(bf16[4,2,2048]{2,1,0:T(2,128)(2,1)S(1)} %get-tuple-element.4.residual_ref, bf16[4,2,3584]{2,1,0:T(2,128)(2,1)S(1)} %get-tuple-element.5.activation_ref), custom_call_target="tpu_custom_call" | custom-call | tf_op jit(solution)/shard_map/pallas_call | solution.py:687

commit v5 on v4

--- a/solution.py
+++ b/solution.py
@@ -309,48 +309,57 @@
         tail = jnp.concatenate([fresh, jnp.zeros((pad, HD), f32)], axis=0) if pad else fresh
         return jnp.concatenate([old.reshape(suffix_rows, HD), tail.astype(bf16)], axis=0)
 
+    def scores_of(first):
+        kv = pl.ds(pl.multiple_of(first // GROUP * HD, HD), HD)
+        pieces = [
+            q8[:, pl.ds(pl.multiple_of((first + g) * HD, HD), HD)] for g in range(unit_heads)
+        ]
+        key_scale = ks8[:, kv]
+        query = jnp.concatenate(pieces, axis=0).astype(bf16)
+        scaled = jnp.concatenate([piece * key_scale for piece in pieces], axis=0).astype(bf16)
+        own_keys = with_fresh(sk_ref[:, :, kv], fk8[:, kv])
+        prefix_scores = lax.dot_general(
+            scaled, pk_ref[:, kv], transposed, preferred_element_type=f32
+        )
+        own_scores = lax.dot_general(query, own_keys, transposed, preferred_element_type=f32)
+        return prefix_scores, own_scores
+
+    def weights_of(prefix_scores, own_scores):
+        prefix_scores = prefix_scores * score_scale
+        own_scores = jnp.where(mask, own_scores * score_scale, masked_score)
+        peak = jnp.maximum(
+            jnp.max(prefix_scores, axis=1, keepdims=True),
+            jnp.max(own_scores, axis=1, keepdims=True),
+        )
+        prefix_weight = jnp.exp(prefix_scores - peak).astype(bf16)
+        own_weight = jnp.where(mask, jnp.exp(own_scores - peak), 0.0).astype(bf16)
+        total = jnp.sum(prefix_weight.astype(f32), axis=1, keepdims=True) + jnp.sum(
+            own_weight.astype(f32), axis=1, keepdims=True
+        )
+        return peak, total, prefix_weight, own_weight
+
+    def values_of(first, prefix_weight, own_weight):
+        kv = pl.ds(pl.multiple_of(first // GROUP * HD, HD), HD)
+        own_values = with_fresh(sv_ref[:, :, kv], fv8[:, kv])
+        value_scale = jnp.concatenate([vs8[:, kv]] * unit_heads, axis=0)
+        prefix_part = jnp.dot(prefix_weight, pv_ref[:, kv], preferred_element_type=f32)
+        own_part = jnp.dot(own_weight, own_values, preferred_element_type=f32)
+        return prefix_part * value_scale + own_part
+
     def attend(b, finish):
+        firsts = [b * heads_block + i * unit_heads for i in range(units)]
+        scores = [scores_of(first) for first in firsts]
+        weights = [weights_of(*score) for score in scores]
+        numerators = [values_of(first, *w[2:]) for first, w in zip(firsts, weights)]
         peaks = jnp.zeros((rs, LANES), f32)
         totals = jnp.ones((rs, LANES), f32)
         for i in range(units):
-            first = b * heads_block + i * unit_heads
-            kv = pl.ds(pl.multiple_of(first // GROUP * HD, HD), HD)
-            pieces = [
-                q8[:, pl.ds(pl.multiple_of((first + g) * HD, HD), HD)] for g in range(unit_heads)
-            ]
-            key_scale = ks8[:, kv]
-            value_scale = vs8[:, kv]
-            query = jnp.concatenate(pieces, axis=0).astype(bf16)
-            scaled = jnp.concatenate([piece * key_scale for piece in pieces], axis=0).astype(bf16)
-            own_keys = with_fresh(sk_ref[:, :, kv], fk8[:, kv])
-            own_values = with_fresh(sv_ref[:, :, kv], fv8[:, kv])
-            prefix_scores = (
-                lax.dot_general(scaled, pk_ref[:, kv], transposed, preferred_element_type=f32)
-                * score_scale
-            )
-            own_scores = (
-                lax.dot_general(query, own_keys, transposed, preferred_element_type=f32)
-                * score_scale
-            )
-            own_scores = jnp.where(mask, own_scores, masked_score)
-            peak = jnp.maximum(
-                jnp.max(prefix_scores, axis=1, keepdims=True),
-                jnp.max(own_scores, axis=1, keepdims=True),
-            )
-            prefix_weight = jnp.exp(prefix_scores - peak).astype(bf16)
-            own_weight = jnp.where(mask, jnp.exp(own_scores - peak), 0.0).astype(bf16)
-            total = jnp.sum(prefix_weight.astype(f32), axis=1, keepdims=True) + jnp.sum(
-                own_weight.astype(f32), axis=1, keepdims=True
-            )
-            numerator = jnp.dot(prefix_weight, pv_ref[:, kv], preferred_element_type=f32)
-            numerator = numerator * jnp.concatenate([value_scale] * unit_heads, axis=0)
-            numerator = numerator + jnp.dot(own_weight, own_values, preferred_element_type=f32)
             for g in range(unit_heads):
                 j = i * unit_heads + g
                 part = slice(g * rs, (g + 1) * rs)
-                peaks = jnp.where(stat_lane == j, peak[part], peaks)
-                totals = jnp.where(stat_lane == j, total[part], totals)
-                acc_s[b, :, j * HD : (j + 1) * HD] = numerator[part].astype(bf16)
+                peaks = jnp.where(stat_lane == j, weights[i][0][part], peaks)
+                totals = jnp.where(stat_lane == j, weights[i][1][part], totals)
+                acc_s[b, :, j * HD : (j + 1) * HD] = numerators[i][part].astype(bf16)
         stat_s[b, 0] = peaks
         stat_s[b, 1] = totals
         finish()
@@ -474,35 +483,42 @@
         up_at = at + everyone
         return jnp.concatenate([product[at : at + rs], product[up_at : up_at + rs]], axis=0)
 
-    def own_unit(g, carry):
-        product = unit_product(g, 2 * everyone)
-        for r in range(row_n):
-            both = gate_and_up(product, 0, r)
-            gate_f[g, r] = both
-            gate_s[g, r] = both.astype(bf16)
-        for d in range(1, row_n):
-            gate_copy(g, d).start()
+    own_step = 2 if own % 2 == 0 else 1
+    shared_step = 2 if shared % 2 == 0 else 1
+
+    def own_units(p, carry):
+        slots = [p * own_step + k for k in range(own_step)]
+        products = [unit_product(g, 2 * everyone) for g in slots]
+        for g, product in zip(slots, products):
+            for r in range(row_n):
+                both = gate_and_up(product, 0, r)
+                gate_f[g, r] = both
+                gate_s[g, r] = both.astype(bf16)
+            for d in range(1, row_n):
+                gate_copy(g, d).start()
         return carry
 
-    def shared_unit(i, carry):
-        product = unit_product(own + i, 2 * split * everyone)
-        for e in range(split):
-            for r in range(row_n):
-                both = gate_and_up(product, e, r)
-                if e == 0:
-                    gate_f[own + i, r] = both
-                gate_s[own + i * split + e, r] = both.astype(bf16)
-        for e, d in others:
-            both_copy(i, e, d).start()
+    def shared_units(p, carry):
+        slots = [p * shared_step + k for k in range(shared_step)]
+        products = [unit_product(own + i, 2 * split * everyone) for i in slots]
+        for i, product in zip(slots, products):
+            for e in range(split):
+                for r in range(row_n):
+                    both = gate_and_up(product, e, r)
+                    if e == 0:
+                        gate_f[own + i, r] = both
+                    gate_s[own + i * split + e, r] = both.astype(bf16)
+            for e, d in others:
+                both_copy(i, e, d).start()
         return carry
 
     landed(gu, gu_sem)
-    lax.fori_loop(0, own, own_unit, 0)
+    lax.fori_loop(0, own // own_step, own_units, 0)
     if split > 1:
         landed(res_g.at[pl.ds(0, split - 1)], pass_sem.at[1])
     for e in range(1, split):
         spread_rows(e, res_g[across(e)].astype(f32).reshape(everyone, depth))
-    lax.fori_loop(0, shared, shared_unit, 0)
+    lax.fori_loop(0, shared // shared_step, shared_units, 0)
 
     square_sum = sq_s[row]
     landed(sq_r, sq_sem.at[1])

time: 34.2 us -> 33.9 us (level)
  no operation moved by 1% of the time
where the time goes in v5:
time: 33.9 us; the launch traced here: 33.7 us
  Pallas kernels  33.1 us (98%)
  between operations  0.64 us (2%)
    pallas_call x1, Pallas kernels, per_device(): pl.pallas_call(functools.partial(layer_kernel, (pre_n, row_n, split, own,...  32.4 us

profile of v5, /device:TPU:0, one launch (start us, length us, event | category | flops | bytes accessed | tf_op | source)
XLA Modules:
  0.0 33.7 jit_solution(7391360119199943108)
XLA Ops:
  0.6 32.4 %shard_map.158 = (bf16[4,2,2048]{2,1,0:T(2,128)(2,1)S(1)}, bf16[4,2,3584]{2,1,0:T(2,128)(2,1)S(1)}) custom-call(s32[4]{0:T(128)} %ids_hbm.1, s32[4]{0:T(128)} %lens_hbm.1, bf16[4,2,8192]{2,1,0:T(2,128)(2,1)} %q_hbm.1, bf16[128,1024]{1,0:T(8,128)(2,1)} %pk_hbm.1, bf16[128,1024]{1,0:T(8,128)(2,1)} %pv_hbm.1, bf16[4,16,1024]{2,1,0:T(8,128)(2,1)} %sk_hbm.1, ...), custom_call_target="tpu_custom_call" | custom-call | tf_op jit(solution)/shard_map/pallas_call | solution.py:669
  33.1 0.7 %shard_map.159 = (bf16[4,2,2048]{2,1,0:T(2,128)(2,1)}, bf16[4,2,3584]{2,1,0:T(2,128)(2,1)}) custom-call(bf16[4,2,2048]{2,1,0:T(2,128)(2,1)S(1)} %get-tuple-element.4.residual_ref, bf16[4,2,3584]{2,1,0:T(2,128)(2,1)S(1)} %get-tuple-element.5.activation_ref), custom_call_target="tpu_custom_call" | custom-call | tf_op jit(solution)/shard_map/pallas_call | solution.py:703

commit v6 on v5

--- a/solution.py
+++ b/solution.py
@@ -14,9 +14,10 @@
 STEPS = 2
 GROUP = HEADS // KV_HEADS
 LANES = 128
-OWN_SHARE = 0.4
-
-GRANT = 40
+UNIT_WIDTHS = (128, 256, 512)
+EARLY_SHARE = 0.3
+
+GRANT = 52
 
 masked_score = -1e30
 f32 = jnp.float32
@@ -80,7 +81,7 @@
     gate_s,
     gate_f,
     gate_r,
-    gate_b,
+    gate_h,
     sq_s,
     sq_r,
     ffn8,
@@ -93,13 +94,10 @@
     mix_sem,
     prod_sem,
     res_sem,
-    pass_sem,
     gate_sem,
-    both_sem,
     sq_sem,
 ):
-    pre_n, row_n, split, own, shared = sizes
-    grp = lax.axis_index("grp")
+    pre_n, row_n, units_ff, early = sizes
     pre = lax.axis_index("pre")
     row = lax.axis_index("row")
     row_local = q_hbm.shape[0]
@@ -119,6 +117,9 @@
     n_tiles = gu.shape[0]
     unit = gate_s.shape[3]
     unit_tiles = unit // LANES
+    halves = 2 if n_out % 2 == 0 else 1
+    half_chunks = n_out // halves
+    half_depth = 2 * depth // halves
     everyone = row_n * rs
 
     gu_rows = gu_hbm.reshape(2 * depth, ff)
@@ -130,15 +131,10 @@
 
     def gu_copy(c):
         return pltpu.make_async_copy(
-            gu_rows.at[:, pl.ds(start(c // unit_tiles) + c % unit_tiles * LANES, LANES)],
+            gu_rows.at[:, pl.ds(c * LANES, LANES)],
             gu.at[c],
             gu_sem,
         )
-
-    def start(slot):
-        if slot < own:
-            return slot * unit
-        return pl.multiple_of((own + grp * shared + slot - own) * unit, LANES)
 
     staged = [
         (ids_hbm, ids_ref),
@@ -180,22 +176,13 @@
             device_id={"row": lax.rem(row + d, row_n)},
             device_id_type=pl.DeviceIdType.MESH,
         )
-    for e in range(1, split):
-        for d in range(row_n):
-            pl.semaphore_signal(
-                barrier,
-                inc=1,
-                device_id={"grp": lax.rem(grp + e, split), "row": lax.rem(row + d, row_n)},
-                device_id_type=pl.DeviceIdType.MESH,
-            )
-
-    def remote(src, dst, sems, axis, target, group=None):
+    def remote(src, dst, sems, axis, target):
         return pltpu.make_async_remote_copy(
             src_ref=src,
             dst_ref=dst,
             send_sem=sems[0],
             recv_sem=sems[1],
-            device_id={axis: target} if group is None else {"grp": group, axis: target},
+            device_id={axis: target},
             device_id_type=pl.DeviceIdType.MESH,
         )
 
@@ -223,16 +210,8 @@
         )
 
     def res_copy(c, d):
-        block_at = res_g.at[grp, pre, :, pl.ds(c * out_width, out_width)]
+        block_at = res_g.at[pre, :, pl.ds(c * out_width, out_width)]
         return remote(block_at, block_at, pair(res_sem, c * (pre_n - 1) + d - 1), "pre", ahead(d))
-
-    def across(e):
-        return lax.rem(grp + e, split)
-
-    def pass_copy(c, e, d):
-        source = lax.rem(pre + pre_n - d, pre_n)
-        block_at = res_g.at[grp, source, :, pl.ds(c * out_width, out_width)]
-        return remote(block_at, block_at, pair(pass_sem), "grp", across(e))
 
     def sq_copy(d):
         return remote(sq_s.at[beside(d)], sq_r.at[d - 1], pair(sq_sem), "row", beside(d))
@@ -241,18 +220,6 @@
         return remote(
             gate_s.at[g, beside(d)], gate_r.at[g, d - 1], pair(gate_sem, g), "row", beside(d)
         )
-
-    def both_copy(i, e, d):
-        return remote(
-            gate_s.at[own + i * split + e, beside(d)],
-            gate_b.at[i, e * row_n + d - 1],
-            pair(both_sem, i),
-            "row",
-            beside(d),
-            across(e) if e > 0 else None,
-        )
-
-    others = [(e, d) for e in range(split) for d in range(row_n) if e + d > 0]
 
     def per_row(ref, shape):
         which = iota(shape, 0) // STEPS
@@ -261,10 +228,8 @@
             out = jnp.where(which == r, ref[r], out)
         return out
 
-    for copy in staged:
+    for copy in staged[:6]:
         copy.wait()
-    for c in range(n_out):
-        ow_copy(c).start()
     adapter = per_row(ids_ref, (rs, 2 * adapters))
     lane = iota((rs, 2 * adapters), 1)
     pick_key = jnp.where(lane == 2 * adapter, 1.0, 0.0)
@@ -370,11 +335,15 @@
         target = jnp.where(2 * pre < pre_n, down, up)
         return lax.rem(target - pre + pre_n, pre_n)
 
+    for copy in staged[6:10]:
+        copy.wait()
+    for c in range(n_out):
+        ow_copy(c).start()
     for k in range(pre_n):
 
         def finish(k=k):
             if k == 0:
-                pl.semaphore_wait(barrier, pre_n + row_n - 2 + (split - 1) * row_n)
+                pl.semaphore_wait(barrier, pre_n + row_n - 2)
             if k < pre_n - 1:
                 stat_copy(farthest(k)).start()
                 acc_copy(farthest(k)).start()
@@ -415,29 +384,23 @@
         return carry
 
     lax.fori_loop(0, n_out, project, 0)
+    for copy in staged[10:]:
+        copy.wait()
     for c in range(n_out):
         part = slice(c * out_width, (c + 1) * out_width)
         value = hid_ref[:, :, part].astype(f32).reshape(hs, out_width) + prod_f[c, pre]
         landed(prod_r.at[c], prod_sem.at[1 + c])
         for d in range(1, pre_n):
             value = value + prod_r[c, d - 1].astype(f32)
-        res_g[grp, pre, :, part] = value.astype(bf16)
+        res_g[pre, :, part] = value.astype(bf16)
         for d in range(1, pre_n):
             res_copy(c, d).start()
-        for e in range(1, split):
-            pass_copy(c, e, 0).start()
         res_out[:, :, part] = value.reshape(hid_local, STEPS, out_width).astype(bf16)
     ffs_copy.wait()
     ffn_pick = jnp.where(
         iota((rs, adapters), 1) == per_row(ids_ref, (rs, adapters)), 1.0, 0.0
     ).astype(bf16)
     ffn8[...] = jnp.dot(ffn_pick, ffs[...], preferred_element_type=f32)
-
-    for c in range(n_out):
-        for d in range(1, pre_n):
-            res_copy(c, d).wait_recv()
-            for e in range(1, split):
-                pass_copy(c, e, d).start()
 
     spread_from = iota((LANES, 4 * LANES), 0)
     spread_to = iota((LANES, 4 * LANES), 1)
@@ -448,77 +411,70 @@
         0.0,
     ).astype(bf16)
 
-    def spread_rows(e, residual):
-        normed = (residual * gain_ref[...].astype(f32).reshape(1, depth)).astype(bf16)
-        first = 2 * e * everyone
-        gate_rows = slice(first, first + everyone)
-        up_rows = slice(first + everyone, first + 2 * everyone)
-        blocks = depth // LANES
-        batch = min(blocks, 4)
-        for j in range(0, blocks, batch):
-            stacked = jnp.concatenate(
-                [normed[:, k * LANES : (k + 1) * LANES] for k in range(j, j + batch)], axis=0
-            )
-            parts = jnp.dot(stacked, spread, preferred_element_type=f32).astype(bf16)
-            for k in range(batch):
-                part = parts[k * everyone : (k + 1) * everyone]
-                at = slice(2 * (j + k) * LANES, 2 * (j + k + 1) * LANES)
-                x_exp[gate_rows, at] = part[:, : 2 * LANES]
-                x_exp[up_rows, at] = part[:, 2 * LANES :]
-
-    residual = res_g[grp].astype(f32).reshape(everyone, depth)
-    squares = jnp.sum(residual * residual, axis=1, keepdims=True)
+    def spread_chunk(c):
+        at = slice(c * out_width, (c + 1) * out_width)
+        residual = res_g[:, :, at].astype(f32).reshape(everyone, out_width)
+        gain = gain_ref[at].astype(f32).reshape(1, out_width)
+        normed = (residual * gain).astype(bf16)
+        blocks = out_width // LANES
+        stacked = jnp.concatenate(
+            [normed[:, k * LANES : (k + 1) * LANES] for k in range(blocks)], axis=0
+        )
+        parts = jnp.dot(stacked, spread, preferred_element_type=f32).astype(bf16)
+        for k in range(blocks):
+            part = parts[k * everyone : (k + 1) * everyone]
+            to = 2 * (c * out_width + k * LANES)
+            x_exp[:everyone, to : to + 2 * LANES] = part[:, : 2 * LANES]
+            x_exp[everyone:, to : to + 2 * LANES] = part[:, 2 * LANES :]
+        return jnp.sum(residual * residual, axis=1, keepdims=True)
+
+    def gather_chunks(first, last):
+        for c in range(first, last):
+            for d in range(1, pre_n):
+                res_copy(c, d).wait_recv()
+        return sum(spread_chunk(c) for c in range(first, last))
+
+    def unit_product(g, first, last):
+        at = slice(first * half_depth, last * half_depth)
+        weights = [gu[g * unit_tiles + t, at] for t in range(unit_tiles)]
+        weight = jnp.concatenate(weights, axis=1) if unit_tiles > 1 else weights[0]
+        return jnp.dot(x_exp[:, at], weight, preferred_element_type=f32)
+
+    def first_half(g, carry):
+        gate_h[g] = unit_product(g, 0, 1)
+        return carry
+
+    def send_unit(g, product):
+        for r in range(row_n):
+            gate = product[r * rs : (r + 1) * rs]
+            up = product[everyone + r * rs : everyone + (r + 1) * rs]
+            both = jnp.concatenate([gate, up], axis=0)
+            gate_f[g, r] = both
+            gate_s[g, r] = both.astype(bf16)
+        for d in range(1, row_n):
+            gate_copy(g, d).start()
+
+    def second_half(g, carry):
+        send_unit(g, gate_h[g] + unit_product(g, 1, 2))
+        return carry
+
+    def whole_unit(g, carry):
+        send_unit(g, unit_product(g, 0, halves))
+        return carry
+
+    squares = gather_chunks(0, half_chunks)
+    landed(gu, gu_sem)
+    if early > 0:
+        lax.fori_loop(0, early, first_half, 0)
+        squares = squares + gather_chunks(half_chunks, n_out)
     for r in range(row_n):
         sq_s[r] = jnp.broadcast_to(squares[r * rs : (r + 1) * rs], (rs, LANES))
     for d in range(1, row_n):
         sq_copy(d).start()
-    spread_rows(0, residual)
-    def unit_product(g, rows):
-        weights = [gu[g * unit_tiles + t] for t in range(unit_tiles)]
-        weight = jnp.concatenate(weights, axis=1) if unit_tiles > 1 else weights[0]
-        return jnp.dot(x_exp[:rows], weight, preferred_element_type=f32)
-
-    def gate_and_up(product, e, r):
-        at = 2 * e * everyone + r * rs
-        up_at = at + everyone
-        return jnp.concatenate([product[at : at + rs], product[up_at : up_at + rs]], axis=0)
-
-    own_step = 2 if own % 2 == 0 else 1
-    shared_step = 2 if shared % 2 == 0 else 1
-
-    def own_units(p, carry):
-        slots = [p * own_step + k for k in range(own_step)]
-        products = [unit_product(g, 2 * everyone) for g in slots]
-        for g, product in zip(slots, products):
-            for r in range(row_n):
-                both = gate_and_up(product, 0, r)
-                gate_f[g, r] = both
-                gate_s[g, r] = both.astype(bf16)
-            for d in range(1, row_n):
-                gate_copy(g, d).start()
-        return carry
-
-    def shared_units(p, carry):
-        slots = [p * shared_step + k for k in range(shared_step)]
-        products = [unit_product(own + i, 2 * split * everyone) for i in slots]
-        for i, product in zip(slots, products):
-            for e in range(split):
-                for r in range(row_n):
-                    both = gate_and_up(product, e, r)
-                    if e == 0:
-                        gate_f[own + i, r] = both
-                    gate_s[own + i * split + e, r] = both.astype(bf16)
-            for e, d in others:
-                both_copy(i, e, d).start()
-        return carry
-
-    landed(gu, gu_sem)
-    lax.fori_loop(0, own // own_step, own_units, 0)
-    if split > 1:
-        landed(res_g.at[pl.ds(0, split - 1)], pass_sem.at[1])
-    for e in range(1, split):
-        spread_rows(e, res_g[across(e)].astype(f32).reshape(everyone, depth))
-    lax.fori_loop(0, shared // shared_step, shared_units, 0)
+    if early > 0:
+        lax.fori_loop(0, early, second_half, 0)
+    for g in range(early, units_ff):
+        whole_unit(g, 0)
 
     square_sum = sq_s[row]
     landed(sq_r, sq_sem.at[1])
@@ -533,7 +489,7 @@
         value = gate / (1.0 + jnp.exp(-gate)) * up * ffn8[:, part]
         act_out[:, :, part] = value.reshape(row_local, STEPS, unit).astype(bf16)
 
-    def finish_own(g, carry):
+    def finish_unit(g, carry):
         landed(gate_r.at[g], gate_sem.at[1 + g])
         both = gate_f[g, row]
         for d in range(1, row_n):
@@ -541,29 +497,15 @@
         activate(both, g * unit)
         return carry
 
-    def finish_shared(i, carry):
-        landed(gate_b.at[i], both_sem.at[1 + i])
-        for e in range(split):
-            both = gate_f[own + i, row] if e == 0 else jnp.zeros((2 * rs, unit), f32)
-            for d in range(1 if e == 0 else 0, row_n):
-                both = both + gate_b[i, e * row_n + d - 1].astype(f32)
-            owner = lax.rem(grp + split - e, split)
-            activate(both, (own + owner * shared + i) * unit)
-        return carry
-
-    lax.fori_loop(0, own, finish_own, 0)
-    lax.fori_loop(0, shared, finish_shared, 0)
+    lax.fori_loop(0, units_ff, finish_unit, 0)
 
     landed(stat_r, stat_sem.at[0])
     landed(acc_r, acc_sem.at[0])
     landed(mix_g.at[pl.ds(0, row_n - 1)], mix_sem.at[0])
     landed(prod_r, prod_sem.at[0])
-    landed(res_g.at[0, pl.ds(0, pre_n - 1)], res_sem.at[0])
-    if split > 1:
-        landed(res_g.at[pl.ds(0, split - 1)], pass_sem.at[0])
+    landed(res_g.at[pl.ds(0, pre_n - 1)], res_sem.at[0])
     landed(sq_r, sq_sem.at[0])
     landed(gate_r, gate_sem.at[0])
-    landed(gate_b, both_sem.at[0])
 
 
 def hand_on(residual_ref, activation_ref, residual_out, activation_out, sem):
@@ -603,12 +545,10 @@
     depth = gate_up.shape[0]
     out_width = min(cols, 512)
     n_out = cols // out_width
-    split = lax.axis_size("grp")
-    unit = 2 * LANES if ff % (2 * LANES) == 0 else LANES
-    units = ff // unit
-    shared = int(units * (1 - OWN_SHARE)) // split
-    own = units - shared * split
-    n_tiles = (own + shared) * unit // LANES
+    unit = max(width for width in UNIT_WIDTHS if ff % width == 0)
+    units_ff = ff // unit
+    early = int(units_ff * EARLY_SHARE) if n_out % 2 == 0 else 0
+    n_tiles = ff // LANES
     everyone = row_n * rs
     dma = pltpu.SemaphoreType.DMA
     vmem = pl.BlockSpec(memory_space=pltpu.VMEM)
@@ -643,12 +583,12 @@
         pltpu.VMEM((n_out, pre_n, hs, out_width), bf16),
         pltpu.VMEM((n_out, pre_n, hs, out_width), f32),
         pltpu.VMEM((n_out, pre_n - 1, hs, out_width), bf16),
-        pltpu.VMEM((split, pre_n, hs, cols), bf16),
-        pltpu.VMEM((2 * split * everyone, 2 * depth), bf16),
-        pltpu.VMEM((own + shared * split, row_n, 2 * rs, unit), bf16),
-        pltpu.VMEM((own + shared, row_n, 2 * rs, unit), f32),
-        pltpu.VMEM((own, row_n - 1, 2 * rs, unit), bf16),
-        pltpu.VMEM((shared, split * row_n - 1, 2 * rs, unit), bf16),
+        pltpu.VMEM((pre_n, hs, cols), bf16),
+        pltpu.VMEM((2 * everyone, 2 * depth), bf16),
+        pltpu.VMEM((units_ff, row_n, 2 * rs, unit), bf16),
+        pltpu.VMEM((units_ff, row_n, 2 * rs, unit), f32),
+        pltpu.VMEM((units_ff, row_n - 1, 2 * rs, unit), bf16),
+        pltpu.VMEM((max(early, 1), 2 * everyone, unit), f32),
         pltpu.VMEM((row_n, rs, LANES), f32),
         pltpu.VMEM((row_n - 1, rs, LANES), f32),
         pltpu.VMEM((rs, ff), f32),
@@ -661,13 +601,11 @@
         dma((2,)),
         dma((1 + n_out,)),
         dma((1 + n_out * (pre_n - 1),)),
-        dma((2,)),
-        dma((1 + own,)),
-        dma((1 + shared,)),
+        dma((1 + units_ff,)),
         dma((2,)),
     ]
     outputs = pl.pallas_call(
-        functools.partial(layer_kernel, (pre_n, row_n, split, own, shared)),
+        functools.partial(layer_kernel, (pre_n, row_n, units_ff, early)),
         out_shape=(
             jax.ShapeDtypeStruct(hidden.shape, bf16),
             jax.ShapeDtypeStruct((row_local, STEPS, ff), bf16),

time: 33.9 us -> 33 us (0.973)
  Pallas kernels: 33.1 us -> 32.2 us
    pallas_call x1, Pallas kernels: 32.4 us -> 31.5 us  [per_device(): pl.pallas_call(functools.partial(layer_kernel, (pre_n, row_n, units_ff, e...]
where the time goes in v6:
time: 33 us; the launch traced here: 32.8 us
  Pallas kernels  32.2 us (98%)
  between operations  0.64 us (2%)
    pallas_call x1, Pallas kernels, per_device(): pl.pallas_call(functools.partial(layer_kernel, (pre_n, row_n, units_ff, e...  31.5 us

profile of v6, /device:TPU:0, one launch (start us, length us, event | category | flops | bytes accessed | tf_op | source)
XLA Modules:
  0.0 32.8 jit_solution(14523719788030473110)
XLA Ops:
  0.6 31.5 %shard_map.158 = (bf16[4,2,2048]{2,1,0:T(2,128)(2,1)S(1)}, bf16[4,2,3584]{2,1,0:T(2,128)(2,1)S(1)}) custom-call(s32[4]{0:T(128)} %ids_hbm.1, s32[4]{0:T(128)} %lens_hbm.1, bf16[4,2,8192]{2,1,0:T(2,128)(2,1)} %q_hbm.1, bf16[128,1024]{1,0:T(8,128)(2,1)} %pk_hbm.1, bf16[128,1024]{1,0:T(8,128)(2,1)} %pv_hbm.1, bf16[4,16,1024]{2,1,0:T(8,128)(2,1)} %sk_hbm.1, ...), custom_call_target="tpu_custom_call" | custom-call | tf_op jit(solution)/shard_map/pallas_call | solution.py:607
  32.2 0.7 %shard_map.159 = (bf16[4,2,2048]{2,1,0:T(2,128)(2,1)}, bf16[4,2,3584]{2,1,0:T(2,128)(2,1)}) custom-call(bf16[4,2,2048]{2,1,0:T(2,128)(2,1)S(1)} %get-tuple-element.4.residual_ref, bf16[4,2,3584]{2,1,0:T(2,128)(2,1)S(1)} %get-tuple-element.5.activation_ref), custom_call_target="tpu_custom_call" | custom-call | tf_op jit(solution)/shard_map/pallas_call | solution.py:641

commit v7 on v6

--- a/solution.py
+++ b/solution.py
@@ -211,7 +211,7 @@
 
     def res_copy(c, d):
         block_at = res_g.at[pre, :, pl.ds(c * out_width, out_width)]
-        return remote(block_at, block_at, pair(res_sem, c * (pre_n - 1) + d - 1), "pre", ahead(d))
+        return remote(block_at, block_at, pair(res_sem, c), "pre", ahead(d))
 
     def sq_copy(d):
         return remote(sq_s.at[beside(d)], sq_r.at[d - 1], pair(sq_sem), "row", beside(d))
@@ -316,17 +316,15 @@
         scores = [scores_of(first) for first in firsts]
         weights = [weights_of(*score) for score in scores]
         numerators = [values_of(first, *w[2:]) for first, w in zip(firsts, weights)]
-        peaks = jnp.zeros((rs, LANES), f32)
-        totals = jnp.ones((rs, LANES), f32)
+        stat = jnp.ones((rs, LANES), f32)
         for i in range(units):
             for g in range(unit_heads):
                 j = i * unit_heads + g
                 part = slice(g * rs, (g + 1) * rs)
-                peaks = jnp.where(stat_lane == j, weights[i][0][part], peaks)
-                totals = jnp.where(stat_lane == j, weights[i][1][part], totals)
+                stat = jnp.where(stat_lane == j, weights[i][0][part], stat)
+                stat = jnp.where(stat_lane == heads_block + j, weights[i][1][part], stat)
                 acc_s[b, :, j * HD : (j + 1) * HD] = numerators[i][part].astype(bf16)
-        stat_s[b, 0] = peaks
-        stat_s[b, 1] = totals
+        stat_s[b] = stat
         finish()
 
     def farthest(k):
@@ -354,8 +352,9 @@
     for c in range(n_tiles):
         gu_copy(c).start()
     landed(stat_r, stat_sem.at[1])
-    peak_of = [stat_s[pre, 0]] + [stat_r[d - 1, 0] for d in range(1, pre_n)]
-    total_of = [stat_s[pre, 1]] + [stat_r[d - 1, 1] for d in range(1, pre_n)]
+    stat_of = [stat_s[pre]] + [stat_r[d - 1] for d in range(1, pre_n)]
+    peak_of = [stat[:, :heads_block] for stat in stat_of]
+    total_of = [stat[:, heads_block : 2 * heads_block] for stat in stat_of]
     highest = functools.reduce(jnp.maximum, peak_of)
     factor_of = [jnp.exp(peak - highest) for peak in peak_of]
     weight_sum = sum(factor * total for factor, total in zip(factor_of, total_of))
@@ -430,8 +429,9 @@
 
     def gather_chunks(first, last):
         for c in range(first, last):
-            for d in range(1, pre_n):
-                res_copy(c, d).wait_recv()
+            landed(
+                res_g.at[pl.ds(0, pre_n - 1), :, pl.ds(0, out_width)], res_sem.at[1 + c]
+            )
         return sum(spread_chunk(c) for c in range(first, last))
 
     def unit_product(g, first, last):
@@ -576,8 +576,8 @@
         pltpu.VMEM((rs, kv_width), f32),
         pltpu.VMEM((pre_n, rs, block), bf16),
         pltpu.VMEM((pre_n - 1, rs, block), bf16),
-        pltpu.VMEM((pre_n, 2, rs, LANES), f32),
-        pltpu.VMEM((pre_n - 1, 2, rs, LANES), f32),
+        pltpu.VMEM((pre_n, rs, LANES), f32),
+        pltpu.VMEM((pre_n - 1, rs, LANES), f32),
         pltpu.VMEM((row_n, rs, block), bf16),
         pltpu.VMEM((everyone, block), bf16),
         pltpu.VMEM((n_out, pre_n, hs, out_width), bf16),
@@ -600,7 +600,7 @@
         dma((2,)),
         dma((2,)),
         dma((1 + n_out,)),
-        dma((1 + n_out * (pre_n - 1),)),
+        dma((1 + n_out,)),
         dma((1 + units_ff,)),
         dma((2,)),
     ]

time: 33 us -> 32.4 us (0.982)
  Pallas kernels: 32.2 us -> 31.6 us
    pallas_call x1, Pallas kernels: 31.5 us -> 31 us  [per_device(): pl.pallas_call(functools.partial(layer_kernel, (pre_n, row_n, units_ff, e...]
where the time goes in v7:
time: 32.4 us; the launch traced here: 32.3 us
  Pallas kernels  31.6 us (98%)
  between operations  0.64 us (2%)
    pallas_call x1, Pallas kernels, per_device(): pl.pallas_call(functools.partial(layer_kernel, (pre_n, row_n, units_ff, e...  31 us
    pallas_call x1, Pallas kernels, per_device(): pl.pallas_call(hand_on, out_shape=tuple((jax.ShapeDtypeStruct(value.shape...  0.65 us

profile of v7, /device:TPU:0, one launch (start us, length us, event | category | flops | bytes accessed | tf_op | source)
XLA Modules:
  0.0 32.3 jit_solution(7145350832428544298)
XLA Ops:
  0.6 31.0 %shard_map.158 = (bf16[4,2,2048]{2,1,0:T(2,128)(2,1)S(1)}, bf16[4,2,3584]{2,1,0:T(2,128)(2,1)S(1)}) custom-call(s32[4]{0:T(128)} %ids_hbm.1, s32[4]{0:T(128)} %lens_hbm.1, bf16[4,2,8192]{2,1,0:T(2,128)(2,1)} %q_hbm.1, bf16[128,1024]{1,0:T(8,128)(2,1)} %pk_hbm.1, bf16[128,1024]{1,0:T(8,128)(2,1)} %pv_hbm.1, bf16[4,16,1024]{2,1,0:T(8,128)(2,1)} %sk_hbm.1, ...), custom_call_target="tpu_custom_call" | custom-call | tf_op jit(solution)/shard_map/pallas_call | solution.py:607
  31.6 0.7 %shard_map.159 = (bf16[4,2,2048]{2,1,0:T(2,128)(2,1)}, bf16[4,2,3584]{2,1,0:T(2,128)(2,1)}) custom-call(bf16[4,2,2048]{2,1,0:T(2,128)(2,1)S(1)} %get-tuple-element.4.residual_ref, bf16[4,2,3584]{2,1,0:T(2,128)(2,1)S(1)} %get-tuple-element.5.activation_ref), custom_call_target="tpu_custom_call" | custom-call | tf_op jit(solution)/shard_map/pallas_call | solution.py:641

commit v8 on v7

--- a/solution.py
+++ b/solution.py
@@ -15,7 +15,7 @@
 GROUP = HEADS // KV_HEADS
 LANES = 128
 UNIT_WIDTHS = (128, 256, 512)
-EARLY_SHARE = 0.3
+EARLY_SHARE = 0.45
 
 GRANT = 52
 
@@ -195,6 +195,18 @@
     def beside(d):
         return lax.rem(row + d, row_n)
 
+    def farthest(at, count):
+        order = []
+        for k in range(count - 1):
+            down = jnp.where(count - 1 - k > at, count - 1 - k, count - 2 - k)
+            up = jnp.where(k < at, k, k + 1)
+            target = jnp.where(2 * at < count, down, up)
+            order.append(lax.rem(target - at + count, count))
+        return order
+
+    far_pre = farthest(pre, pre_n)
+    far_row = farthest(row, row_n)
+
     def acc_copy(d):
         return remote(acc_s.at[ahead(d)], acc_r.at[d - 1], pair(acc_sem), "pre", ahead(d))
 
@@ -327,12 +339,6 @@
         stat_s[b] = stat
         finish()
 
-    def farthest(k):
-        down = jnp.where(pre_n - 1 - k > pre, pre_n - 1 - k, pre_n - 2 - k)
-        up = jnp.where(k < pre, k, k + 1)
-        target = jnp.where(2 * pre < pre_n, down, up)
-        return lax.rem(target - pre + pre_n, pre_n)
-
     for copy in staged[6:10]:
         copy.wait()
     for c in range(n_out):
@@ -343,10 +349,10 @@
             if k == 0:
                 pl.semaphore_wait(barrier, pre_n + row_n - 2)
             if k < pre_n - 1:
-                stat_copy(farthest(k)).start()
-                acc_copy(farthest(k)).start()
-
-        attend(ahead(farthest(k)) if k < pre_n - 1 else pre, finish)
+                stat_copy(far_pre[k]).start()
+                acc_copy(far_pre[k]).start()
+
+        attend(ahead(far_pre[k]) if k < pre_n - 1 else pre, finish)
 
     ffs_copy.start()
     for c in range(n_tiles):
@@ -366,7 +372,7 @@
         for d in range(1, pre_n):
             value = value + acc_r[d - 1, :, part].astype(f32) * factor_of[d][:, j : j + 1]
         mix_g[row, :, part] = value.astype(bf16)
-    for d in range(1, row_n):
+    for d in far_row:
         mix_copy(d).start()
     landed(ow, ow_sem)
     landed(mix_g.at[pl.ds(0, row_n - 1)], mix_sem.at[1])
@@ -378,7 +384,7 @@
             part = product[p * hs : (p + 1) * hs]
             prod_f[c, p] = part
             prod_s[c, p] = part.astype(bf16)
-        for d in range(1, pre_n):
+        for d in far_pre:
             prod_copy(c, d).start()
         return carry
 
@@ -392,7 +398,7 @@
         for d in range(1, pre_n):
             value = value + prod_r[c, d - 1].astype(f32)
         res_g[pre, :, part] = value.astype(bf16)
-        for d in range(1, pre_n):
+        for d in far_pre:
             res_copy(c, d).start()
         res_out[:, :, part] = value.reshape(hid_local, STEPS, out_width).astype(bf16)
     ffs_copy.wait()
@@ -451,7 +457,7 @@
             both = jnp.concatenate([gate, up], axis=0)
             gate_f[g, r] = both
             gate_s[g, r] = both.astype(bf16)
-        for d in range(1, row_n):
+        for d in far_row:
             gate_copy(g, d).start()
 
     def second_half(g, carry):

time: 32.4 us -> 32.3 us (level)
  no operation moved by 1% of the time
where the time goes in v8:
time: 32.3 us; the launch traced here: 32.2 us
  Pallas kernels  31.5 us (98%)
  between operations  0.64 us (2%)
    pallas_call x1, Pallas kernels, per_device(): pl.pallas_call(functools.partial(layer_kernel, (pre_n, row_n, units_ff, e...  30.9 us
    pallas_call x1, Pallas kernels, per_device(): pl.pallas_call(hand_on, out_shape=tuple((jax.ShapeDtypeStruct(value.shape...  0.65 us

profile of v8, /device:TPU:0, one launch (start us, length us, event | category | flops | bytes accessed | tf_op | source)
XLA Modules:
  0.0 32.2 jit_solution(11528637739593381733)
XLA Ops:
  0.6 30.9 %shard_map.158 = (bf16[4,2,2048]{2,1,0:T(2,128)(2,1)S(1)}, bf16[4,2,3584]{2,1,0:T(2,128)(2,1)S(1)}) custom-call(s32[4]{0:T(128)} %ids_hbm.1, s32[4]{0:T(128)} %lens_hbm.1, bf16[4,2,8192]{2,1,0:T(2,128)(2,1)} %q_hbm.1, bf16[128,1024]{1,0:T(8,128)(2,1)} %pk_hbm.1, bf16[128,1024]{1,0:T(8,128)(2,1)} %pv_hbm.1, bf16[4,16,1024]{2,1,0:T(8,128)(2,1)} %sk_hbm.1, ...), custom_call_target="tpu_custom_call" | custom-call | tf_op jit(solution)/shard_map/pallas_call | solution.py:613
  31.5 0.7 %shard_map.159 = (bf16[4,2,2048]{2,1,0:T(2,128)(2,1)}, bf16[4,2,3584]{2,1,0:T(2,128)(2,1)}) custom-call(bf16[4,2,2048]{2,1,0:T(2,128)(2,1)S(1)} %get-tuple-element.4.residual_ref, bf16[4,2,3584]{2,1,0:T(2,128)(2,1)S(1)} %get-tuple-element.5.activation_ref), custom_call_target="tpu_custom_call" | custom-call | tf_op jit(solution)/shard_map/pallas_call | solution.py:647

commit v9 on v8

--- a/solution.py
+++ b/solution.py
@@ -503,7 +503,8 @@
         activate(both, g * unit)
         return carry
 
-    lax.fori_loop(0, units_ff, finish_unit, 0)
+    for g in range(units_ff):
+        finish_unit(g, 0)
 
     landed(stat_r, stat_sem.at[0])
     landed(acc_r, acc_sem.at[0])

time: 32.3 us -> 32.3 us (level)
  no operation moved by 1% of the time
where the time goes in v9:
time: 32.3 us; the launch traced here: 32.1 us
  Pallas kernels  31.5 us (98%)
  between operations  0.64 us (2%)
    pallas_call x1, Pallas kernels, per_device(): pl.pallas_call(functools.partial(layer_kernel, (pre_n, row_n, units_ff, e...  30.8 us
    pallas_call x1, Pallas kernels, per_device(): pl.pallas_call(hand_on, out_shape=tuple((jax.ShapeDtypeStruct(value.shape...  0.65 us

profile of v9, /device:TPU:0, one launch (start us, length us, event | category | flops | bytes accessed | tf_op | source)
XLA Modules:
  0.0 32.1 jit_solution(5905025374178203712)
XLA Ops:
  0.6 30.8 %shard_map.158 = (bf16[4,2,2048]{2,1,0:T(2,128)(2,1)S(1)}, bf16[4,2,3584]{2,1,0:T(2,128)(2,1)S(1)}) custom-call(s32[4]{0:T(128)} %ids_hbm.1, s32[4]{0:T(128)} %lens_hbm.1, bf16[4,2,8192]{2,1,0:T(2,128)(2,1)} %q_hbm.1, bf16[128,1024]{1,0:T(8,128)(2,1)} %pk_hbm.1, bf16[128,1024]{1,0:T(8,128)(2,1)} %pv_hbm.1, bf16[4,16,1024]{2,1,0:T(8,128)(2,1)} %sk_hbm.1, ...), custom_call_target="tpu_custom_call" | custom-call | tf_op jit(solution)/shard_map/pallas_call | solution.py:614
  31.5 0.7 %shard_map.159 = (bf16[4,2,2048]{2,1,0:T(2,128)(2,1)}, bf16[4,2,3584]{2,1,0:T(2,128)(2,1)}) custom-call(bf16[4,2,2048]{2,1,0:T(2,128)(2,1)S(1)} %get-tuple-element.4.residual_ref, bf16[4,2,3584]{2,1,0:T(2,128)(2,1)S(1)} %get-tuple-element.5.activation_ref), custom_call_target="tpu_custom_call" | custom-call | tf_op jit(solution)/shard_map/pallas_call | solution.py:648
